TPU v7x, 32 devices: a whole 2x2x4 slice. The times are simulated.
32 devices in a mesh: gz: 2 (over x), gy: 4 (over y, core), gx: 4 (over z).
Axes of the slice: x: 2, y: 2, z: 4, core: 2. Of those that a mesh axis runs over, the one named last changes fastest.
Arguments:
- pressure: float32 [8, 512, 512], P('gz', 'gy', 'gx'), may hold values from -6 to 6
- light: float32 [4, 3], replicated, may hold values from -4 to 4
- palette: float32 [3, 2], replicated, may hold values from -4 to 4
- rate: float32 [4], replicated, may hold values from 0.0625 to 0.375
- shear: int32 [4, 8, 2], replicated, may hold values from 0 to 8
- offset: int32 [4, 2, 2], replicated, may hold values from 0 to 31
- order: int32 [4, 2], replicated, may hold values from 0 to 1, each once within a row
Outputs:
- picture: float32 [4, 4, 2, 256, 512], P(None, None, 'gz', 'gy', 'gx')
Inputs may be any that keep to these rules, and one draw needn't show every extreme that they name: `order`: each row is a permutation of 0 to 1.
All inputs are finite; a program needn't handle non-finite values.
Results may differ from a plain program's by a relative error of at most 0.00005.
Values sent between devices are 32-bit elements; how exact they have to be, the bound alone decides.
A program may use at most 64 MiB of HBM per device.

v0:
```python
import functools
import math

import jax
import jax.numpy as jnp
from jax import lax
from jax.experimental import pallas as pl
from jax.experimental.pallas import tpu as pltpu
from jax.sharding import PartitionSpec as P

VIEWS = 4
SHEAR = 8
REACH = 32
HALO = SHEAR + REACH
SUB = 8
BLOCK = 16
LANES = 128
MESH = pl.DeviceIdType.MESH


def padded(cells, sides, width):
    for axis, dim in sides:
        count = lax.axis_size(axis)
        ends = count - 1
        head = lax.slice_in_dim(cells, 0, width, axis=dim)
        tail = lax.slice_in_dim(cells, cells.shape[dim] - width, cells.shape[dim], axis=dim)
        cells = jnp.concatenate(
            [
                lax.ppermute(tail, axis, [(i, (i + 1) % count) for i in range(ends)]),
                cells,
                lax.ppermute(head, axis, [((i + 1) % count, i) for i in range(ends)]),
            ],
            axis=dim,
        )
    return cells


def shifted(value, axis, steps):
    count = lax.axis_size(axis)
    first, last = (max(0, -steps), min(count, count - steps))
    return lax.ppermute(value, axis, [(source, source + steps) for source in range(first, last)])


def surface_terms(slab):
    inner = slab[1:-1, 1:-1, 1:-1]
    grad_depth = 0.5 * (slab[2:, 1:-1, 1:-1] - slab[:-2, 1:-1, 1:-1])
    grad_rows = 0.5 * (slab[1:-1, 2:, 1:-1] - slab[1:-1, :-2, 1:-1])
    grad_cols = 0.5 * (slab[1:-1, 1:-1, 2:] - slab[1:-1, 1:-1, :-2])
    factor = lax.rsqrt(
        grad_depth * grad_depth + grad_rows * grad_rows + grad_cols * grad_cols + 1.0
    )
    return (inner, (grad_depth * factor, grad_rows * factor, grad_cols * factor))


def render_layers(inner, normals, shifts, light, palette, rate, rows, cols):
    lengths = jnp.sqrt(jnp.sum(light * light, axis=1, keepdims=True) + 1.0)
    towards = light / lengths
    offsets = palette[:, 0][:, None, None]
    slopes = palette[:, 1][:, None, None]
    layers = []
    for view in range(light.shape[0]):

        def advance(carry, items):
            color, depth = carry
            value_slab, normal_depth, normal_rows, normal_cols, moved = items
            start = (SHEAR - moved[0], SHEAR - moved[1])
            value = lax.dynamic_slice(value_slab, start, (rows, cols))
            dot = (
                lax.dynamic_slice(normal_depth, start, (rows, cols)) * towards[view, 0]
                + lax.dynamic_slice(normal_rows, start, (rows, cols)) * towards[view, 1]
                + lax.dynamic_slice(normal_cols, start, (rows, cols)) * towards[view, 2]
            )
            shade = 0.25 + 0.75 * dot * dot
            density = rate[view] * (1.0 + jnp.tanh(value))
            alpha = 1.0 - jnp.exp(-density)
            weight = alpha * jnp.exp(-depth)
            hues = jax.nn.sigmoid(offsets + slopes * value[None]) * shade[None]
            return ((color + hues * weight[None], depth + density), None)

        start_carry = (
            jnp.zeros((3, rows, cols), jnp.float32),
            jnp.zeros((rows, cols), jnp.float32),
        )
        (color, depth), _ = lax.scan(
            advance, start_carry, (inner, normals[0], normals[1], normals[2], shifts[view])
        )
        layers.append(jnp.concatenate([color, depth[None]], axis=0))
    return jnp.stack(layers)


def precedence(order):
    bricks = order.shape[1]
    onehot = (order[:, :, None] == jnp.arange(bricks, dtype=jnp.int32)[None, None, :]).astype(
        jnp.float32
    )
    ranks = jnp.sum(onehot * jnp.arange(bricks, dtype=jnp.float32)[None, :, None], axis=1)
    return (ranks[:, None, :] < ranks[:, :, None]).astype(jnp.float32)


def many_bricks(pressure, light, palette, rate, shear, offset, order):
    depth_cells, rows, cols = pressure.shape
    brick = lax.axis_index("gz")
    zero = jnp.zeros((), jnp.int32)
    widened = padded(pressure, (("gy", 1), ("gx", 2)), SHEAR + 1)
    slab = padded(widened, (("gz", 0),), 1)
    inner, normals = surface_terms(slab)
    shifts = lax.dynamic_slice(shear, (zero, brick * depth_cells, zero), (VIEWS, depth_cells, 2))
    layers = render_layers(inner, normals, shifts, light, palette, rate, rows, cols)
    moved = lax.dynamic_index_in_dim(offset, brick, 1, keepdims=False)
    blank = jnp.zeros((4, rows + REACH, cols + REACH), jnp.float32)
    canvas = jnp.stack(
        [
            lax.dynamic_update_slice(blank, layers[view], (zero, moved[view, 0], moved[view, 1]))
            for view in range(VIEWS)
        ]
    )
    own_tile = canvas[:, :, :rows, :cols]
    from_above = shifted(canvas[:, :, rows:, :cols], "gy", 1)
    from_left = shifted(canvas[:, :, :rows, cols:], "gx", 1)
    from_diagonal = shifted(canvas[:, :, rows:, cols:], ("gy", "gx"), lax.axis_size("gx") + 1)
    from_diagonal = from_diagonal * (lax.axis_index("gx") > 0).astype(jnp.float32)
    own_tile = own_tile.at[:, :, :REACH, :].add(from_above)
    own_tile = own_tile.at[:, :, :, :REACH].add(from_left)
    own_tile = own_tile.at[:, :, :REACH, :REACH].add(from_diagonal)
    ranking = precedence(order)
    pieces = lax.all_to_all(own_tile[None], "gz", split_axis=3, concat_axis=0, tiled=True)
    depths = pieces[:, :, 3]
    cover = jnp.einsum("vbc,cvyx->bvyx", ranking, depths, precision=lax.Precision.HIGHEST)
    colors = jnp.sum(pieces[:, :, :3] * jnp.exp(-cover)[:, :, None], axis=0)
    opacity = 1.0 - jnp.exp(-jnp.sum(depths, axis=0))
    image = jnp.concatenate([colors, opacity[:, None]], axis=1)
    return image[:, :, None]


def segments(tall):
    return (0, HALO, tall - HALO)


def exchange(
    dims, mine, here, p_ref, m_ref, full_in, rest_in, ends_in, full_out, rest_out, ends_out, sends,
    arrivals, local_sem,
):
    ny, nx, bz, rows = dims
    z, y, x = here
    strip = rows // 2
    tall = HALO + strip + SUB
    per = LANES // HALO
    groups = -(-bz // per)
    other = 1 - mine
    first_lane = LANES - HALO
    has_up, has_down = y > 0, y < ny - 1
    has_left, has_right = x > 0, x < nx - 1

    def remote(src, dst, slot, arrival, who):
        return pltpu.make_async_remote_copy(
            src_ref=src,
            dst_ref=dst,
            send_sem=sends.at[slot],
            recv_sem=arrivals.at[arrival],
            device_id=who,
            device_id_type=MESH,
        )

    def spans(to):
        if to == 0:
            return pl.ds(0, strip + SUB), pl.ds(HALO, strip + SUB)
        return pl.ds(strip - HALO, HALO + strip), pl.ds(0, HALO + strip)

    def main(brick, g):
        count = min(per, bz - g * per)
        source, target = spans(1 - brick)
        return remote(
            p_ref.at[pl.ds(g * per, count), source],
            m_ref.at[pl.ds(1 + brick * bz + g * per, count), target],
            g, g, (1 - z, y, x),
        )

    def down(brick):
        return remote(
            p_ref.at[:, pl.ds(rows - HALO, HALO)],
            m_ref.at[pl.ds(1 + brick * bz, bz), pl.ds(0, HALO)],
            groups, groups + brick, (0, y + 1, x),
        )

    def up(brick):
        return remote(
            p_ref.at[:, pl.ds(0, SUB)],
            m_ref.at[pl.ds(1 + brick * bz, bz), pl.ds(HALO + strip, SUB)],
            groups + 1, groups + brick, (1, y - 1, x),
        )

    def rightward(brick, g):
        slot = groups + 2 + brick * groups + g
        if g == groups - 1:
            return remote(rest_out.at[brick], rest_in.at[brick], slot, slot, (z, y, x + 1))
        at = brick * (groups - 1) + g
        return remote(full_out.at[at], full_in.at[at], slot, slot, (z, y, x + 1))

    def leftward(brick):
        slot = 3 * groups + 2 + brick
        return remote(ends_out.at[brick], ends_in.at[brick], slot, slot, (z, y, x - 1))

    def started(there, copy):
        @pl.when(there)
        def _():
            copy.start()

    def arrived(there, copy):
        @pl.when(there)
        def _():
            copy.wait_recv()

    def left(there, copy):
        @pl.when(there)
        def _():
            copy.wait_send()

    def pack(brick, g):
        if g == groups - 1:
            lane = lax.broadcasted_iota(jnp.int32, (HALO, LANES), 1)
            pieces = [m_ref[brick * bz + bz, row : row + HALO] for row in segments(tall)]
        else:
            lane = lax.broadcasted_iota(jnp.int32, (tall, LANES), 1)
            pieces = [m_ref[1 + brick * bz + g * per + j] for j in range(per)]
        packed = pltpu.roll(pieces[0], LANES - first_lane, 1)
        for j in range(1, per):
            moved = pltpu.roll(pieces[j], (j * HALO - first_lane) % LANES, 1)
            packed = jnp.where(lane >= j * HALO, moved, packed)
        if g == groups - 1:
            rest_out[brick] = packed
        else:
            full_out[brick * (groups - 1) + g] = packed

    def pack_ends(brick):
        lane = lax.broadcasted_iota(jnp.int32, (BLOCK, LANES), 1)
        ends = jnp.zeros((BLOCK, LANES), jnp.float32)
        for j in range(bz):
            for i in range(tall // BLOCK):
                at = i * bz + j
                cells = m_ref[1 + brick * bz + j, i * BLOCK : (i + 1) * BLOCK]
                ends = jnp.where(lane == at, pltpu.roll(cells, at, 1) if at else cells, ends)
        ends_out[brick] = ends

    def halo_in(brick):
        if mine == 0:
            arrived(has_up, down(brick))
        else:
            arrived(has_down, up(brick))

    def own():
        source, target = spans(mine)
        return pltpu.make_async_copy(
            p_ref.at[:, source], m_ref.at[pl.ds(1 + mine * bz, bz), target], local_sem
        )

    def open_up():
        for g in range(groups):
            main(mine, g).start()
        started(has_down, down(mine))
        started(has_up, up(mine))
        own().wait()
        halo_in(mine)
        for g in range(groups):
            pack(mine, g)
            started(has_right, rightward(mine, g))
        pack_ends(mine)
        started(has_left, leftward(mine))
        halo_in(other)
        for g in range(groups):
            main(other, g).wait_recv()
            pack(other, g)
            started(has_right, rightward(other, g))
        pack_ends(other)
        started(has_left, leftward(other))

    def columns_in(brick):
        for g in range(groups):
            arrived(has_left, rightward(brick, g))
        arrived(has_right, leftward(brick))

    def close():
        for g in range(groups):
            main(mine, g).wait_send()
        left(has_down, down(mine))
        left(has_up, up(mine))
        for brick in range(2):
            for g in range(groups):
                left(has_right, rightward(brick, g))
            left(has_left, leftward(brick))

    return open_up, columns_in, close, own


def render(
    dims, light_in, palette_in, rate_in, shear_in, offset_in, order_in, p_ref, out_ref,
    light, palette, rate, shear, offset, order, m_ref, full_in, rest_in, ends_in,
    full_out, rest_out, ends_out, h_ref, r_ref, dm, dh, sends, arrivals, local_sem, table_sems,
):
    ny, nx, bz, rows = dims
    strip = rows // 2
    tall = HALO + strip + SUB
    depth = 2 * bz
    per = LANES // HALO
    groups = -(-bz // per)
    first_lane = LANES - HALO
    z, y, x = lax.axis_index("gz"), lax.axis_index("gy"), lax.axis_index("gx")
    has_up, has_down = y > 0, y < ny - 1
    has_left, has_right = x > 0, x < nx - 1

    tables = [
        pltpu.make_async_copy(source, target, table_sems.at[i])
        for i, (source, target) in enumerate(
            (
                (light_in, light), (palette_in, palette), (rate_in, rate),
                (shear_in, shear), (offset_in, offset), (order_in, order),
            )
        )
    ]
    cross = y + 2 * z - 1
    partners = (
        (y >= 0, (1 - z, y, x)),
        (has_up, (z, y - 1, x)),
        (has_down, (z, y + 1, x)),
        (jnp.logical_and(cross >= 0, cross < ny), (1 - z, cross, x)),
        (has_left, (z, y, x - 1)),
        (has_right, (z, y, x + 1)),
    )
    barrier = pltpu.get_barrier_semaphore()
    count = 0
    for there, who in partners:

        @pl.when(there)
        def _():
            pl.semaphore_signal(barrier, inc=1, device_id=who, device_id_type=MESH)

        count = count + there.astype(jnp.int32)
    steps = [
        exchange(
            dims, mine, (z, y, x), p_ref, m_ref, full_in, rest_in, ends_in, full_out, rest_out,
            ends_out, sends, arrivals, local_sem,
        )
        for mine in range(2)
    ]

    for mine in range(2):

        @pl.when(z == mine)
        def _():
            steps[mine][3]().start()

    for copy in tables:
        copy.start()

    empty = jnp.zeros((tall, LANES), jnp.float32)
    for ref in (m_ref, h_ref):
        ref[0] = empty
        ref[depth + 1] = empty

    @pl.when(jnp.logical_and(z == 0, y == 0))
    def _():
        m_ref[:, :HALO] = jnp.zeros((depth + 2, HALO, LANES), jnp.float32)

    @pl.when(jnp.logical_and(z == 1, y == ny - 1))
    def _():
        m_ref[:, HALO + strip :] = jnp.zeros((depth + 2, SUB, LANES), jnp.float32)

    @pl.when(x == 0)
    def _():
        full_in[...] = jnp.zeros(full_in.shape, jnp.float32)
        rest_in[...] = jnp.zeros(rest_in.shape, jnp.float32)

    @pl.when(x == nx - 1)
    def _():
        ends_in[...] = jnp.zeros(ends_in.shape, jnp.float32)

    pl.semaphore_wait(barrier, count)

    for mine in range(2):

        @pl.when(z == mine)
        def _():
            steps[mine][0]()
            steps[mine][1](mine)

    def unpack(brick):
        for j in range(bz - 1):
            shift = (first_lane - (j % per) * HALO) % LANES
            cells = full_in[brick * (groups - 1) + j // per]
            h_ref[1 + brick * bz + j] = pltpu.roll(cells, shift, 1)
        cells = rest_in[brick]
        for j, row in enumerate(segments(tall)):
            moved = pltpu.roll(cells, (first_lane - j * HALO) % LANES, 1)
            h_ref[brick * bz + bz, row : row + HALO] = moved
        cells = ends_in[brick]
        for i in range(tall // BLOCK):
            moved = pltpu.roll(cells, (LANES - 1 - i * bz) % LANES, 1)
            r_ref[brick, i * BLOCK : (i + 1) * BLOCK] = moved

    for copy in tables:
        copy.wait()

    towards = []
    for w in range(VIEWS):
        a, b, c = light[w, 0], light[w, 1], light[w, 2]
        inverse = lax.rsqrt(jnp.full((SUB, LANES), a * a + b * b + c * c + 1.0, jnp.float32))
        towards.append((a * inverse, b * inverse, c * inverse))

    lane = lax.broadcasted_iota(jnp.int32, (SUB, LANES), 1)
    last = lane == LANES - 1
    first = lane == 0

    def slopes(k, carry):
        for i in range((HALO + strip) // SUB):
            top = i * SUB
            here = m_ref[k + 1, top + 1 : top + 1 + SUB]
            side = h_ref[k + 1, top + 1 : top + 1 + SUB]
            beyond = pltpu.roll(
                r_ref[k // bz, top + 1 : top + 1 + SUB], (LANES - k % bz) % LANES, 1
            )
            here_r, here_l = pltpu.roll(here, LANES - 1, 1), pltpu.roll(here, 1, 1)
            side_r, side_l = pltpu.roll(side, LANES - 1, 1), pltpu.roll(side, 1, 1)
            for ref, cols, dots in (
                (m_ref, jnp.where(last, beyond, here_r) - jnp.where(first, side_l, here_l), dm),
                (h_ref, jnp.where(last, here_r, side_r) - side_l, dh),
            ):
                deep = ref[k + 2, top + 1 : top + 1 + SUB] - ref[k, top + 1 : top + 1 + SUB]
                down = ref[k + 1, top + 2 : top + 2 + SUB] - ref[k + 1, top : top + SUB]
                half = 0.5 * lax.rsqrt(0.25 * (deep * deep + down * down + cols * cols) + 1.0)
                deep, down, cols = deep * half, down * half, cols * half
                for w in range(VIEWS):
                    a, b, c = towards[w]
                    dots[w, k, top : top + SUB] = deep * a + down * b + cols * c
        return carry

    unpack(z)
    lax.fori_loop(z * (bz + 1), z * (bz + 1) + bz - 1, slopes, 0)

    for mine in range(2):

        @pl.when(z == mine)
        def _():
            steps[mine][1](1 - mine)
            steps[mine][2]()

    unpack(1 - z)
    lax.fori_loop((1 - z) * (bz - 1), (1 - z) * (bz - 1) + bz + 1, slopes, 0)

    tile = 32
    base_row = y * rows + z * strip
    base_col = x * LANES
    lanes = lax.broadcasted_iota(jnp.int32, (tile, LANES), 1)
    rows_at = lax.broadcasted_iota(jnp.int32, (tile, LANES), 0)
    bias = [0.5 * palette[0, c] for c in range(3)]
    gain = [0.5 * palette[1, c] for c in range(3)]

    def view_part(step, carry):
        w = step // (strip // tile)
        top = (step % (strip // tile)) * tile
        through = jnp.ones((tile, LANES), jnp.float32)
        ambient = jnp.zeros((tile, LANES), jnp.float32)
        colors = [jnp.zeros((tile, LANES), jnp.float32) for _ in range(3)]
        rate2 = rate[w] * (-math.log2(math.e))
        for place in range(2):
            brick = order[place, w]
            off_r, off_c = offset[brick, 0, w], offset[brick, 1, w]
            inside = jnp.logical_and(
                rows_at >= off_r - base_row - top, lanes >= off_c - base_col
            )
            fall = jnp.where(inside, rate2, 0.0)
            for j in range(bz):
                k = brick * bz + j
                sr = off_r + shear[w, 0, k]
                sc = off_c + shear[w, 1, k]
                at = HALO + top - sr
                wrap = lanes >= LANES - sc
                value = jnp.where(
                    wrap, h_ref[k + 1, pl.ds(at, tile)], m_ref[k + 1, pl.ds(at, tile)]
                )
                dot = jnp.where(wrap, dh[w, k, pl.ds(at - 1, tile)], dm[w, k, pl.ds(at - 1, tile)])
                value = pltpu.roll(value, sc, 1)
                dot = pltpu.roll(dot, sc, 1)
                kept = jnp.exp2(fall * (1.0 + jnp.tanh(value)))
                weight = (0.125 + 0.375 * dot * dot) * ((1.0 - kept) * through)
                through = through * kept
                ambient = ambient + weight
                for c in range(3):
                    colors[c] = colors[c] + weight * jnp.tanh(bias[c] + gain[c] * value)
        for c in range(3):
            out_ref[w, c, pl.ds(top, tile)] = ambient + colors[c]
        out_ref[w, 3, pl.ds(top, tile)] = 1.0 - through
        return carry

    lax.fori_loop(0, VIEWS * (strip // tile), view_part, 0)


def two_bricks(mesh, pressure, light, palette, rate, shear, offset, order):
    bz, rows, cols = pressure.shape
    dims = (mesh.shape["gy"], mesh.shape["gx"], bz, rows)
    strip = rows // 2
    tall = HALO + strip + SUB
    depth = 2 * bz
    groups = -(-bz // (LANES // HALO))
    vmem = pl.BlockSpec(memory_space=pltpu.VMEM)
    hbm = pl.BlockSpec(memory_space=pltpu.HBM)
    f32 = jnp.float32
    copies = 3 * groups + 4
    tables = (
        light,
        palette.T,
        rate,
        jnp.transpose(shear, (0, 2, 1)),
        jnp.transpose(offset, (1, 2, 0)),
        order.T,
    )
    image = pl.pallas_call(
        functools.partial(render, dims),
        out_shape=jax.ShapeDtypeStruct((VIEWS, 4, strip, LANES), f32),
        in_specs=[hbm] * 7,
        out_specs=vmem,
        scratch_shapes=[
            *[pltpu.SMEM(table.shape, table.dtype) for table in tables],
            pltpu.VMEM((depth + 2, tall, LANES), f32),
            pltpu.VMEM((2 * groups - 2, tall, LANES), f32),
            pltpu.VMEM((2, HALO, LANES), f32),
            pltpu.VMEM((2, BLOCK, LANES), f32),
            pltpu.VMEM((2 * groups - 2, tall, LANES), f32),
            pltpu.VMEM((2, HALO, LANES), f32),
            pltpu.VMEM((2, BLOCK, LANES), f32),
            pltpu.VMEM((depth + 2, tall, LANES), f32),
            pltpu.VMEM((2, tall, LANES), f32),
            pltpu.VMEM((VIEWS, depth, HALO + strip, LANES), f32),
            pltpu.VMEM((VIEWS, depth, HALO + strip, LANES), f32),
            pltpu.SemaphoreType.DMA((copies,)),
            pltpu.SemaphoreType.DMA((copies,)),
            pltpu.SemaphoreType.DMA,
            pltpu.SemaphoreType.DMA((len(tables),)),
        ],
        compiler_params=pltpu.CompilerParams(collective_id=0, has_side_effects=True, vmem_limit_bytes=12 << 20),
        name="render",
    )(
        *[pltpu.with_memory_space_constraint(t, pltpu.HBM) for t in (*tables, pressure)]
    )
    return image[:, :, None]


def fits(mesh, shape):
    bz, rows, cols = shape
    tall = HALO + rows // 2 + SUB
    return (
        mesh.shape["gz"] == 2
        and cols == LANES
        and rows % 64 == 0
        and 2 * HALO <= tall <= 3 * HALO
        and tall % BLOCK == 0
        and bz % (LANES // HALO) == 1
        and bz * (tall // BLOCK) <= LANES
    )


def on_device(mesh, pressure, *rest):
    if fits(mesh, pressure.shape):
        return two_bricks(mesh, pressure, *rest)
    return many_bricks(pressure, *rest)


def solution(mesh):
    return jax.shard_map(
        functools.partial(on_device, mesh),
        mesh=mesh,
        in_specs=(P("gz", "gy", "gx"), P(), P(), P(), P(), P(), P()),
        out_specs=P(None, None, "gz", "gy", "gx"),
        check_vma=False,
    )
```

profile of v0, /device:TPU:0, one launch (start us, length us, event | category | flops | bytes accessed | tf_op | source)
XLA Modules:
  0.0 16.7 jit_solution(4798860076905697595)
XLA Ops:
  0.0 15.9 %render.1 = f32[4,4,64,128]{3,2,1,0:T(8,128)S(1)} custom-call(f32[4,3]{1,0:T(4,128)} %light_in.1, f32[2,3]{1,0:T(2,128)} %bitcast.10, f32[4]{0:T(128)} %rate_in.1, s32[4,2,8]{2,1,0:T(2,128)} %bitcast.8, s32[2,2,4]{2,1,0:T(2,128)} %bitcast.9, s32[2,4]{1,0:T(2,128)} %bitcast.11, f32[4,128,128]{2,1,0:T(8,128)} %p_ref.1), custom_call_target="tpu_custom_call" | custom-call | tf_op jit(solution)/shard_map/render/pallas_call | solution.py:515
  16.0 0.8 %copy.10 = f32[4,4,1,64,128]{4,3,2,1,0:T(8,128)} copy(f32[4,4,1,64,128]{4,3,2,1,0:T(8,128)S(1)} %bitcast.7) | data formatting | bytes 1048576
where the time goes:
time: 16.9 us; the launch traced here: 16.7 us
  Pallas kernels  15.9 us (94%)
  local copies, waits for them, and re-layouts  0.8 us (5%)
    pallas_call x1, Pallas kernels, two_bricks(): pl.pallas_call(functools.partial(render, dims), out_shape=jax.ShapeDtypeS...  15.9 us
    unnamed x1, local copies, waits for them, and re-layouts  0.8 us

commit v1 on v0

v1 whole, which is shorter than its diff:
```python
import functools
import math

import jax
import jax.numpy as jnp
from jax import lax
from jax.experimental import pallas as pl
from jax.experimental.pallas import tpu as pltpu
from jax.sharding import PartitionSpec as P

VIEWS = 4
SHEAR = 8
REACH = 32
HALO = SHEAR + REACH
SUB = 8
LANES = 128
MESH = pl.DeviceIdType.MESH


def padded(cells, sides, width):
    for axis, dim in sides:
        count = lax.axis_size(axis)
        ends = count - 1
        head = lax.slice_in_dim(cells, 0, width, axis=dim)
        tail = lax.slice_in_dim(cells, cells.shape[dim] - width, cells.shape[dim], axis=dim)
        cells = jnp.concatenate(
            [
                lax.ppermute(tail, axis, [(i, (i + 1) % count) for i in range(ends)]),
                cells,
                lax.ppermute(head, axis, [((i + 1) % count, i) for i in range(ends)]),
            ],
            axis=dim,
        )
    return cells


def shifted(value, axis, steps):
    count = lax.axis_size(axis)
    first, last = (max(0, -steps), min(count, count - steps))
    return lax.ppermute(value, axis, [(source, source + steps) for source in range(first, last)])


def surface_terms(slab):
    inner = slab[1:-1, 1:-1, 1:-1]
    grad_depth = 0.5 * (slab[2:, 1:-1, 1:-1] - slab[:-2, 1:-1, 1:-1])
    grad_rows = 0.5 * (slab[1:-1, 2:, 1:-1] - slab[1:-1, :-2, 1:-1])
    grad_cols = 0.5 * (slab[1:-1, 1:-1, 2:] - slab[1:-1, 1:-1, :-2])
    factor = lax.rsqrt(
        grad_depth * grad_depth + grad_rows * grad_rows + grad_cols * grad_cols + 1.0
    )
    return (inner, (grad_depth * factor, grad_rows * factor, grad_cols * factor))


def render_layers(inner, normals, shifts, light, palette, rate, rows, cols):
    lengths = jnp.sqrt(jnp.sum(light * light, axis=1, keepdims=True) + 1.0)
    towards = light / lengths
    offsets = palette[:, 0][:, None, None]
    slopes = palette[:, 1][:, None, None]
    layers = []
    for view in range(light.shape[0]):

        def advance(carry, items):
            color, depth = carry
            value_slab, normal_depth, normal_rows, normal_cols, moved = items
            start = (SHEAR - moved[0], SHEAR - moved[1])
            value = lax.dynamic_slice(value_slab, start, (rows, cols))
            dot = (
                lax.dynamic_slice(normal_depth, start, (rows, cols)) * towards[view, 0]
                + lax.dynamic_slice(normal_rows, start, (rows, cols)) * towards[view, 1]
                + lax.dynamic_slice(normal_cols, start, (rows, cols)) * towards[view, 2]
            )
            shade = 0.25 + 0.75 * dot * dot
            density = rate[view] * (1.0 + jnp.tanh(value))
            alpha = 1.0 - jnp.exp(-density)
            weight = alpha * jnp.exp(-depth)
            hues = jax.nn.sigmoid(offsets + slopes * value[None]) * shade[None]
            return ((color + hues * weight[None], depth + density), None)

        start_carry = (
            jnp.zeros((3, rows, cols), jnp.float32),
            jnp.zeros((rows, cols), jnp.float32),
        )
        (color, depth), _ = lax.scan(
            advance, start_carry, (inner, normals[0], normals[1], normals[2], shifts[view])
        )
        layers.append(jnp.concatenate([color, depth[None]], axis=0))
    return jnp.stack(layers)


def precedence(order):
    bricks = order.shape[1]
    onehot = (order[:, :, None] == jnp.arange(bricks, dtype=jnp.int32)[None, None, :]).astype(
        jnp.float32
    )
    ranks = jnp.sum(onehot * jnp.arange(bricks, dtype=jnp.float32)[None, :, None], axis=1)
    return (ranks[:, None, :] < ranks[:, :, None]).astype(jnp.float32)


def many_bricks(pressure, light, palette, rate, shear, offset, order):
    depth_cells, rows, cols = pressure.shape
    brick = lax.axis_index("gz")
    zero = jnp.zeros((), jnp.int32)
    widened = padded(pressure, (("gy", 1), ("gx", 2)), SHEAR + 1)
    slab = padded(widened, (("gz", 0),), 1)
    inner, normals = surface_terms(slab)
    shifts = lax.dynamic_slice(shear, (zero, brick * depth_cells, zero), (VIEWS, depth_cells, 2))
    layers = render_layers(inner, normals, shifts, light, palette, rate, rows, cols)
    moved = lax.dynamic_index_in_dim(offset, brick, 1, keepdims=False)
    blank = jnp.zeros((4, rows + REACH, cols + REACH), jnp.float32)
    canvas = jnp.stack(
        [
            lax.dynamic_update_slice(blank, layers[view], (zero, moved[view, 0], moved[view, 1]))
            for view in range(VIEWS)
        ]
    )
    own_tile = canvas[:, :, :rows, :cols]
    from_above = shifted(canvas[:, :, rows:, :cols], "gy", 1)
    from_left = shifted(canvas[:, :, :rows, cols:], "gx", 1)
    from_diagonal = shifted(canvas[:, :, rows:, cols:], ("gy", "gx"), lax.axis_size("gx") + 1)
    from_diagonal = from_diagonal * (lax.axis_index("gx") > 0).astype(jnp.float32)
    own_tile = own_tile.at[:, :, :REACH, :].add(from_above)
    own_tile = own_tile.at[:, :, :, :REACH].add(from_left)
    own_tile = own_tile.at[:, :, :REACH, :REACH].add(from_diagonal)
    ranking = precedence(order)
    pieces = lax.all_to_all(own_tile[None], "gz", split_axis=3, concat_axis=0, tiled=True)
    depths = pieces[:, :, 3]
    cover = jnp.einsum("vbc,cvyx->bvyx", ranking, depths, precision=lax.Precision.HIGHEST)
    colors = jnp.sum(pieces[:, :, :3] * jnp.exp(-cover)[:, :, None], axis=0)
    opacity = 1.0 - jnp.exp(-jnp.sum(depths, axis=0))
    image = jnp.concatenate([colors, opacity[:, None]], axis=1)
    return image[:, :, None]


class Route:
    def __init__(self, dims, side, step, start, count, slab, half):
        bz = dims[2]
        self.side, self.step, self.half = side, step, half
        self.rows, self.slab = pl.ds(start, count), pl.ds(slab, count)
        self.groups = LANES // (SUB * bz)
        self.tiles = range(start // SUB, (start + count) // SUB)
        self.first = slab // SUB
        self.folds = range(
            self.tiles[0] // self.groups, self.tiles[-1] // self.groups + 1
        )
        self.size = (len(self.tiles) + len(self.folds)) * SUB
        self.base = self.sent = 0

    def there(self, y, ny):
        return y + self.step >= 0 if self.step < 0 else y + self.step < ny

    def comes(self, y, ny):
        return y - self.step < ny if self.step < 0 else y - self.step >= 0

    def wide(self, tile):
        return (tile - self.tiles[0]) * SUB

    def narrow(self, fold):
        return (len(self.tiles) + fold - self.folds[0]) * SUB


def routes_of(dims):
    rows = dims[3]
    strip = rows // 2
    routes = [
        Route(dims, 0, 0, 0, strip + SUB, HALO, 0),
        Route(dims, 0, 1, rows - HALO, HALO, 0, 1),
        Route(dims, 1, 0, strip - HALO, HALO + strip, 0, 0),
        Route(dims, 1, -1, 0, SUB, HALO + strip, 1),
    ]
    sent = 0
    for route in routes:
        route.sent = sent
        sent += route.size
    routes[1].base, routes[3].base = routes[0].size, routes[2].size
    return routes, sent, max(routes[0].size + routes[1].size, routes[2].size + routes[3].size)


MAIN, EDGE, BESIDE, COLS, ENDS, SLOTS = 0, 2, 4, 5, 9, 13


def exchange(
    dims, mine, here, p_ref, m_ref, cols_out, cols_in, ends_out, ends_in, sends, arrivals
):
    ny, nx, bz, rows = dims
    z, y, x = here
    has_left, has_right = x > 0, x < nx - 1
    routes = routes_of(dims)[0]

    def remote(src, dst, sent, arrival, who):
        return pltpu.make_async_remote_copy(
            src_ref=src,
            dst_ref=dst,
            send_sem=sends.at[sent],
            recv_sem=arrivals.at[arrival],
            device_id=who,
            device_id_type=MESH,
        )

    def part(brick, late):
        near = bz // 2 if late is None else bz - bz // 2
        if late is None:
            return 0, bz
        return (near, bz - near) if (brick == 1) == late else (0, near)

    def rows_of(brick, route, late):
        start, count = part(brick, late)
        slot = BESIDE if late is None else (EDGE if route.half else MAIN) + int(late)
        return remote(
            p_ref.at[pl.ds(start, count), route.rows],
            m_ref.at[pl.ds(1 + brick * bz + start, count), route.slab],
            slot, slot, (route.side, y + route.step, x),
        )

    def cols_of(brick, route):
        return remote(
            cols_out.at[pl.ds(route.sent, route.size)],
            cols_in.at[brick, pl.ds(route.base, route.size)],
            COLS + 2 * route.side + route.half, COLS + 2 * brick + route.half,
            (route.side, y + route.step, x + 1),
        )

    def ends_of(brick, route):
        return remote(
            ends_out,
            ends_in.at[brick, route.half],
            ENDS + 2 * route.side + route.half, ENDS + 2 * brick + route.half,
            (route.side, y + route.step, x - 1),
        )

    def both(a, b):
        return jnp.logical_and(a, b)

    def outgoing(same, kinds):
        for route in routes:
            if (route.side == mine) != same:
                continue
            there = route.there(y, ny)
            for kind in kinds:
                if kind == "cols":
                    yield both(there, has_right), cols_of(mine, route)
                elif kind == "ends":
                    yield both(there, has_left), ends_of(mine, route)
                elif not same:
                    yield there, rows_of(mine, route, kind == "late")
                elif route.half:
                    yield there, rows_of(mine, route, None)

    def incoming(brick, kinds):
        for route in routes:
            if route.side != mine:
                continue
            comes = route.comes(y, ny)
            for kind in kinds:
                if kind == "cols":
                    yield both(comes, has_left), cols_of(brick, route)
                elif kind == "ends":
                    yield both(comes, has_right), ends_of(brick, route)
                elif brick != mine:
                    yield comes, rows_of(brick, route, kind == "late")
                elif route.half:
                    yield comes, rows_of(brick, route, None)

    def apply(pairs, act):
        for there, copy in pairs:

            @pl.when(there)
            def _():
                act(copy)

    def send(same, *kinds):
        apply(outgoing(same, kinds), lambda copy: copy.start())

    def receive(brick, *kinds):
        apply(incoming(brick, kinds), lambda copy: copy.wait_recv())

    def close():
        apply(outgoing(True, ("early", "cols", "ends")), lambda copy: copy.wait_send())
        apply(outgoing(False, ("early", "late", "cols", "ends")), lambda copy: copy.wait_send())

    return send, receive, close


def partners_of(dims, here):
    ny, nx = dims[:2]
    z, y, x = here
    cross = 2 * z - 1
    for side, step in ((z, -1), (z, 0), (z, 1), (1 - z, 0), (1 - z, cross)):
        for over in (-1, 0, 1):
            if side is z and isinstance(step, int) and step == 0 and over == 0:
                continue
            there = jnp.logical_and(
                jnp.logical_and(y + step >= 0, y + step < ny),
                jnp.logical_and(x + over >= 0, x + over < nx),
            )
            yield there, (side, y + step, x + over)


def render(
    dims, light_in, palette_in, rate_in, shear_in, offset_in, order_in, p_ref, out_ref,
    light, palette, rate, shear, offset, order, tile_ref, m_ref, own_ref, cols_in, ends_in,
    cols_out, ends_out, h_ref, r_ref, dm, dh, back, sends, arrivals, local_sems, table_sems,
):
    ny, nx, bz, rows = dims
    strip = rows // 2
    tall = HALO + strip + SUB
    depth = 2 * bz
    blocks = (HALO + strip) // SUB
    wide_lanes = HALO - SUB
    z, y, x = lax.axis_index("gz"), lax.axis_index("gy"), lax.axis_index("gx")
    routes = routes_of(dims)[0]

    tables = [
        pltpu.make_async_copy(source, target, table_sems.at[i])
        for i, (source, target) in enumerate(
            (
                (light_in, light), (palette_in, palette), (rate_in, rate),
                (shear_in, shear), (offset_in, offset), (order_in, order),
            )
        )
    ]
    barrier = pltpu.get_barrier_semaphore()

    def sided(act):
        for mine in range(2):

            @pl.when(z == mine)
            def _():
                act(mine)

    count = 0
    for there, who in partners_of(dims, (z, y, x)):

        @pl.when(there)
        def _():
            pl.semaphore_signal(barrier, inc=1, device_id=who, device_id_type=MESH)

        count = count + there.astype(jnp.int32)

    steps = [
        exchange(
            dims, mine, (z, y, x), p_ref, m_ref, cols_out, cols_in, ends_out, ends_in,
            sends, arrivals,
        )
        for mine in range(2)
    ]

    def local_slab(mine):
        route = routes[2 * mine]
        return pltpu.make_async_copy(
            p_ref.at[:, route.rows], m_ref.at[pl.ds(1 + mine * bz, bz), route.slab],
            local_sems.at[1],
        )

    local_tile = pltpu.make_async_copy(p_ref, tile_ref, local_sems.at[0])
    local_tile.start()
    sided(lambda mine: local_slab(mine).start())
    for copy in tables:
        copy.start()

    empty = jnp.zeros((tall, LANES), jnp.float32)
    for ref in (m_ref, h_ref):
        ref[0] = empty
        ref[depth + 1] = empty

    def blank(mine):
        route = routes[2 * mine + 1]

        @pl.when(jnp.logical_not(route.comes(y, ny)))
        def _():
            m_ref[:, route.slab] = jnp.zeros((depth + 2, len(route.tiles) * SUB, LANES), jnp.float32)
            cols_in[:, route.base : route.base + route.size] = jnp.zeros(
                (2, route.size, LANES), jnp.float32
            )
            ends_in[:, 1] = jnp.zeros((2, SUB, LANES), jnp.float32)

    sided(blank)

    @pl.when(x == 0)
    def _():
        cols_in[...] = jnp.zeros(cols_in.shape, jnp.float32)

    @pl.when(x == nx - 1)
    def _():
        ends_in[...] = jnp.zeros(ends_in.shape, jnp.float32)

    lane = lax.broadcasted_iota(jnp.int32, (SUB, LANES), 1)
    last = lane == LANES - 1
    first = lane == 0
    groups = routes[0].groups
    tiles = rows // SUB

    def cell(j, t):
        return tile_ref[j, t * SUB : (t + 1) * SUB]

    def put(t_or_fold, is_wide, value):
        for route in routes:
            if t_or_fold in (route.tiles if is_wide else route.folds):
                at = route.sent + (route.wide if is_wide else route.narrow)(t_or_fold)
                cols_out[at : at + SUB] = value

    def merged(pieces):
        while len(pieces) > 1:
            pieces = [
                (a[0], jnp.where(lane >= b[0], b[1], a[1]))
                for a, b in zip(pieces[::2], pieces[1::2])
            ] + (pieces[-1:] if len(pieces) % 2 else [])
        return pieces[0][1]

    def turned(value, by):
        return pltpu.roll(value, by % LANES, 1) if by % LANES else value

    local_tile.wait()
    for t in range(tiles):
        put(
            t, True,
            merged(
                [(wide_lanes * j, turned(cell(j, t), wide_lanes * (j + 1))) for j in range(bz)]
            ),
        )
    for fold in range(tiles // groups):
        put(
            fold, False,
            merged(
                [
                    (
                        SUB * (bz * g + j),
                        turned(cell(j, fold * groups + g), SUB * (bz * g + j) + HALO),
                    )
                    for g in range(groups)
                    for j in range(bz)
                ]
            ),
        )
    ends_out[...] = merged(
        [(t * bz + j, turned(cell(j, t), t * bz + j)) for t in range(tiles) for j in range(bz)]
    )

    def unpack(mine, brick):
        for route in routes[2 * mine : 2 * mine + 2]:
            for t in route.tiles:
                row = (route.first + t - route.tiles[0]) * SUB
                at = route.base + route.wide(t)
                wide = cols_in[brick, at : at + SUB]
                at = route.base + route.narrow(t // groups)
                narrow = cols_in[brick, at : at + SUB]
                for j in range(bz):
                    h_ref[1 + brick * bz + j, row : row + SUB] = jnp.where(
                        lane >= LANES - wide_lanes,
                        turned(wide, -wide_lanes * (j + 1)),
                        turned(narrow, -SUB * (bz * (t % groups) + j) - HALO),
                    )
                r_ref[brick, row : row + SUB] = turned(
                    ends_in[brick, route.half], LANES - 1 - t * bz
                )

    pl.semaphore_wait(barrier, count)

    def opening(mine):
        send, receive, close = steps[mine]
        send(False, "early", "cols", "ends")
        send(True, "early", "cols", "ends")
        local_slab(mine).wait()
        receive(mine, "early", "cols", "ends")
        send(False, "late")
        own_ref[...] = m_ref[1 + mine * bz : 1 + (mine + 1) * bz]
        unpack(mine, mine)

    def middle(mine):
        send, receive, close = steps[mine]
        receive(1 - mine, "early", "cols", "ends")
        unpack(mine, 1 - mine)

    def ending(mine):
        send, receive, close = steps[mine]
        receive(1 - mine, "late")

    sided(opening)
    for copy in tables:
        copy.wait()

    towards = []
    for w in range(VIEWS):
        a, b, c = light[w, 0], light[w, 1], light[w, 2]
        inverse = lax.rsqrt(jnp.full((SUB, LANES), a * a + b * b + c * c + 1.0, jnp.float32))
        towards.append((a * inverse, b * inverse, c * inverse))

    def slopes(k, carry):
        for i in range(blocks):
            top = i * SUB
            here = m_ref[k + 1, top + 1 : top + 1 + SUB]
            side = h_ref[k + 1, top + 1 : top + 1 + SUB]
            beyond = pltpu.roll(
                r_ref[k // bz, top + 1 : top + 1 + SUB], (LANES - k % bz) % LANES, 1
            )
            here_r, here_l = pltpu.roll(here, LANES - 1, 1), pltpu.roll(here, 1, 1)
            side_r, side_l = pltpu.roll(side, LANES - 1, 1), pltpu.roll(side, 1, 1)
            for ref, cols, dots in (
                (m_ref, jnp.where(last, beyond, here_r) - jnp.where(first, side_l, here_l), dm),
                (h_ref, jnp.where(last, here_r, side_r) - side_l, dh),
            ):
                deep = ref[k + 2, top + 1 : top + 1 + SUB] - ref[k, top + 1 : top + 1 + SUB]
                down = ref[k + 1, top + 2 : top + 2 + SUB] - ref[k + 1, top : top + SUB]
                half = 0.5 * lax.rsqrt(0.25 * (deep * deep + down * down + cols * cols) + 1.0)
                deep, down, cols = deep * half, down * half, cols * half
                for w in range(VIEWS):
                    a, b, c = towards[w]
                    dots[w, k, top : top + SUB] = deep * a + down * b + cols * c
        return carry

    tile = 32
    per_view = strip // tile
    base_row = y * rows + z * strip
    base_col = x * LANES
    lanes = lax.broadcasted_iota(jnp.int32, (tile, LANES), 1)
    rows_at = lax.broadcasted_iota(jnp.int32, (tile, LANES), 0)
    bias = [0.5 * palette[0, c] for c in range(3)]
    gain = [0.5 * palette[1, c] for c in range(3)]

    def march(w, top, brick, cells, start, colors, through):
        ambient = jnp.zeros((tile, LANES), jnp.float32)
        rate2 = rate[w] * (-math.log2(math.e))
        off_r, off_c = offset[brick, 0, w], offset[brick, 1, w]
        inside = jnp.logical_and(rows_at >= off_r - base_row - top, lanes >= off_c - base_col)
        fall = jnp.where(inside, rate2, 0.0)
        for j in range(bz):
            k = brick * bz + j
            sr = off_r + shear[w, 0, k]
            sc = off_c + shear[w, 1, k]
            at = HALO + top - sr
            wrap = lanes >= LANES - sc
            value = jnp.where(wrap, h_ref[k + 1, pl.ds(at, tile)], cells[start + j, pl.ds(at, tile)])
            dot = jnp.where(wrap, dh[w, k, pl.ds(at - 1, tile)], dm[w, k, pl.ds(at - 1, tile)])
            value = pltpu.roll(value, sc, 1)
            dot = pltpu.roll(dot, sc, 1)
            kept = jnp.exp2(fall * (1.0 + jnp.tanh(value)))
            weight = (0.125 + 0.375 * dot * dot) * ((1.0 - kept) * through)
            through = through * kept
            ambient = ambient + weight
            colors = [
                colors[c] + weight * jnp.tanh(bias[c] + gain[c] * value) for c in range(3)
            ]
        return [color + ambient for color in colors], through

    def views(act):
        def one(step, carry):
            act(step // per_view, (step % per_view) * tile)
            return carry

        lax.fori_loop(0, VIEWS * per_view, one, 0)

    def own_layer(w, top):
        at = pl.ds(top, tile)
        zero = jnp.zeros((tile, LANES), jnp.float32)
        colors, through = march(w, top, z, own_ref, 0, [zero] * 3, zero + 1.0)
        ahead = order[0, w] == z
        for c in range(3):
            out_ref[w, c, at] = jnp.where(ahead, colors[c], 0.0)
            back[w, c, at] = jnp.where(ahead, 0.0, colors[c])
        out_ref[w, 3, at] = jnp.where(ahead, through, 1.0)
        back[w, 3, at] = jnp.where(ahead, 1.0, through)

    def other_layer(w, top):
        at = pl.ds(top, tile)
        colors, through = march(
            w, top, 1 - z, m_ref, 1 + (1 - z) * bz, [out_ref[w, c, at] for c in range(3)],
            out_ref[w, 3, at],
        )
        for c in range(3):
            out_ref[w, c, at] = colors[c] + through * back[w, c, at]
        out_ref[w, 3, at] = 1.0 - through * back[w, 3, at]

    def each(start, stop):
        lax.fori_loop(start, stop, slopes, 0)

    each(z * (bz + 1), z * (bz + 1) + bz - 1)
    sided(middle)
    each(bz - 1, bz + 1)
    views(own_layer)
    sided(ending)
    each((1 - z) * (bz + 1), (1 - z) * (bz + 1) + bz - 1)
    views(other_layer)
    sided(lambda mine: steps[mine][2]())


def two_bricks(mesh, pressure, light, palette, rate, shear, offset, order):
    bz, rows, cols = pressure.shape
    dims = (mesh.shape["gy"], mesh.shape["gx"], bz, rows)
    strip = rows // 2
    tall = HALO + strip + SUB
    depth = 2 * bz
    vmem = pl.BlockSpec(memory_space=pltpu.VMEM)
    hbm = pl.BlockSpec(memory_space=pltpu.HBM)
    f32 = jnp.float32
    _, sent, got = routes_of(dims)
    tables = (
        light,
        palette.T,
        rate,
        jnp.transpose(shear, (0, 2, 1)),
        jnp.transpose(offset, (1, 2, 0)),
        order.T,
    )
    image = pl.pallas_call(
        functools.partial(render, dims),
        out_shape=jax.ShapeDtypeStruct((VIEWS, 4, strip, LANES), f32),
        in_specs=[hbm] * 7,
        out_specs=vmem,
        scratch_shapes=[
            *[pltpu.SMEM(table.shape, table.dtype) for table in tables],
            pltpu.VMEM((bz, rows, LANES), f32),
            pltpu.VMEM((depth + 2, tall, LANES), f32),
            pltpu.VMEM((bz, tall, LANES), f32),
            pltpu.VMEM((2, got, LANES), f32),
            pltpu.VMEM((2, 2, SUB, LANES), f32),
            pltpu.VMEM((sent, LANES), f32),
            pltpu.VMEM((SUB, LANES), f32),
            pltpu.VMEM((depth + 2, tall, LANES), f32),
            pltpu.VMEM((2, tall, LANES), f32),
            pltpu.VMEM((VIEWS, depth, HALO + strip, LANES), f32),
            pltpu.VMEM((VIEWS, depth, HALO + strip, LANES), f32),
            pltpu.VMEM((VIEWS, 4, strip, LANES), f32),
            pltpu.SemaphoreType.DMA((SLOTS,)),
            pltpu.SemaphoreType.DMA((SLOTS,)),
            pltpu.SemaphoreType.DMA((2,)),
            pltpu.SemaphoreType.DMA((len(tables),)),
        ],
        compiler_params=pltpu.CompilerParams(collective_id=0, has_side_effects=True, vmem_limit_bytes=12 << 20),
        name="render",
    )(
        *[pltpu.with_memory_space_constraint(t, pltpu.HBM) for t in (*tables, pressure)]
    )
    return image[:, :, None]


def fits(mesh, shape):
    bz, rows, cols = shape
    return (
        mesh.shape["gz"] == 2
        and cols == LANES
        and rows % 64 == 0
        and 2 * HALO <= rows <= LANES
        and bz * (HALO - SUB) == LANES
        and bz * (rows // SUB) <= LANES
    )


def on_device(mesh, pressure, *rest):
    if fits(mesh, pressure.shape):
        return two_bricks(mesh, pressure, *rest)
    return many_bricks(pressure, *rest)


def solution(mesh):
    return jax.shard_map(
        functools.partial(on_device, mesh),
        mesh=mesh,
        in_specs=(P("gz", "gy", "gx"), P(), P(), P(), P(), P(), P()),
        out_specs=P(None, None, "gz", "gy", "gx"),
        check_vma=False,
    )
```

time: 16.9 us -> 15.2 us (0.90)
  the two profiles are of different devices: /device:TPU:0 before, /device:TPU:19 now
where the time goes in v1:
time: 15.2 us; the launch traced here: 15.1 us
  Pallas kernels  14.3 us (94%)
  local copies, waits for them, and re-layouts  0.8 us (5%)
    pallas_call x1, Pallas kernels, two_bricks(): pl.pallas_call(functools.partial(render, dims), out_shape=jax.ShapeDtypeS...  14.3 us
    unnamed x1, local copies, waits for them, and re-layouts  0.8 us

profile of v1, /device:TPU:19, one launch (start us, length us, event | category | flops | bytes accessed | tf_op | source)
XLA Modules:
  0.0 15.1 jit_solution(2984085667922464605)
XLA Ops:
  0.0 14.3 %render.1 = f32[4,4,64,128]{3,2,1,0:T(8,128)S(1)} custom-call(f32[4,3]{1,0:T(4,128)} %light_in.1, f32[2,3]{1,0:T(2,128)} %bitcast.10, f32[4]{0:T(128)} %rate_in.1, s32[4,2,8]{2,1,0:T(2,128)} %bitcast.8, s32[2,2,4]{2,1,0:T(2,128)} %bitcast.9, s32[2,4]{1,0:T(2,128)} %bitcast.11, f32[4,128,128]{2,1,0:T(8,128)} %p_ref.1), custom_call_target="tpu_custom_call" | custom-call | tf_op jit(solution)/shard_map/render/pallas_call | solution.py:603
  14.3 0.8 %copy.10 = f32[4,4,1,64,128]{4,3,2,1,0:T(8,128)} copy(f32[4,4,1,64,128]{4,3,2,1,0:T(8,128)S(1)} %bitcast.7) | data formatting | bytes 1048576

commit v2 on v1

--- a/solution.py
+++ b/solution.py
@@ -175,15 +175,18 @@
     return routes, sent, max(routes[0].size + routes[1].size, routes[2].size + routes[3].size)
 
 
-MAIN, EDGE, BESIDE, COLS, ENDS, SLOTS = 0, 2, 4, 5, 9, 13
+MAIN, EDGE, BESIDE, COLS, ENDS, SLOTS = 0, 3, 6, 7, 11, 15
+PARTS = 3
+FACING, BELOW, RIGHT, ACROSS = range(4)
 
 
 def exchange(
-    dims, mine, here, p_ref, m_ref, cols_out, cols_in, ends_out, ends_in, sends, arrivals
+    dims, mine, here, p_ref, m_ref, cols_out, cols_in, ends_out, ends_in, sends, arrivals, ready
 ):
     ny, nx, bz, rows = dims
     z, y, x = here
     has_left, has_right = x > 0, x < nx - 1
+    has_up, has_down = y > 0, y < ny - 1
     routes = routes_of(dims)[0]
 
     def remote(src, dst, sent, arrival, who):
@@ -196,15 +199,12 @@
             device_id_type=MESH,
         )
 
-    def part(brick, late):
-        near = bz // 2 if late is None else bz - bz // 2
-        if late is None:
-            return 0, bz
-        return (near, bz - near) if (brick == 1) == late else (0, near)
-
-    def rows_of(brick, route, late):
-        start, count = part(brick, late)
-        slot = BESIDE if late is None else (EDGE if route.half else MAIN) + int(late)
+    def rows_of(brick, route, part):
+        start = 0 if part is None else part
+        count = bz if part is None else (bz - part if part == PARTS - 1 else 1)
+        if part is not None and brick == 0:
+            start = bz - start - count
+        slot = BESIDE if part is None else (EDGE if route.half else MAIN) + part
         return remote(
             p_ref.at[pl.ds(start, count), route.rows],
             m_ref.at[pl.ds(1 + brick * bz + start, count), route.slab],
@@ -227,78 +227,125 @@
             (route.side, y + route.step, x - 1),
         )
 
-    def both(a, b):
-        return jnp.logical_and(a, b)
-
-    def outgoing(same, kinds):
-        for route in routes:
-            if (route.side == mine) != same:
-                continue
-            there = route.there(y, ny)
-            for kind in kinds:
-                if kind == "cols":
-                    yield both(there, has_right), cols_of(mine, route)
-                elif kind == "ends":
-                    yield both(there, has_left), ends_of(mine, route)
-                elif not same:
-                    yield there, rows_of(mine, route, kind == "late")
-                elif route.half:
-                    yield there, rows_of(mine, route, None)
-
-    def incoming(brick, kinds):
+    def rows_out(route):
+        there = route.there(y, ny)
+        if route.side != mine:
+            return [(there, rows_of(mine, route, part)) for part in range(PARTS)]
+        return [(there, rows_of(mine, route, None))] if route.half else []
+
+    def cols_sent(same):
+        return [
+            (jnp.logical_and(r.there(y, ny), has_right), cols_of(mine, r))
+            for r in routes
+            if (r.side == mine) == same
+        ]
+
+    def ends_sent():
+        return [(jnp.logical_and(r.there(y, ny), has_left), ends_of(mine, r)) for r in routes]
+
+    def apply(pairs, act):
+        for there, copy in pairs:
+
+            @pl.when(there)
+            def _():
+                act(copy)
+
+    def start(pairs):
+        apply(pairs, lambda copy: copy.start())
+
+    def heard(kind, there, count):
+        @pl.when(there)
+        def _():
+            pl.semaphore_wait(ready.at[kind], count)
+
+    mains, own_halo, halos = (
+        (routes[2], routes[1], routes[3]) if mine == 0 else (routes[0], routes[3], routes[1])
+    )
+    next_ones = [1 + there.astype(jnp.int32) for there in (has_down, has_up)]
+
+    def send_first():
+        if mine == 0:
+            start(rows_out(halos))
+        else:
+            start(rows_out(mains))
+            start(rows_out(own_halo))
+
+    def send_rest():
+        if mine == 0:
+            heard(FACING, y >= 0, 1)
+            start(rows_out(mains))
+            start(ends_sent())
+            heard(BELOW, has_down, 1)
+            start(rows_out(own_halo))
+        else:
+            start(ends_sent())
+            heard(BELOW, has_down, 1)
+            start(rows_out(halos))
+        heard(RIGHT, has_right, next_ones[mine])
+        start(cols_sent(True))
+        heard(ACROSS, has_right, next_ones[1 - mine])
+        apply(cols_sent(True), lambda copy: copy.wait_send())
+        start(cols_sent(False))
+
+    def receive(brick, parts, sides):
+        pairs = []
         for route in routes:
             if route.side != mine:
                 continue
             comes = route.comes(y, ny)
-            for kind in kinds:
-                if kind == "cols":
-                    yield both(comes, has_left), cols_of(brick, route)
-                elif kind == "ends":
-                    yield both(comes, has_right), ends_of(brick, route)
-                elif brick != mine:
-                    yield comes, rows_of(brick, route, kind == "late")
-                elif route.half:
-                    yield comes, rows_of(brick, route, None)
-
-    def apply(pairs, act):
-        for there, copy in pairs:
-
-            @pl.when(there)
-            def _():
-                act(copy)
-
-    def send(same, *kinds):
-        apply(outgoing(same, kinds), lambda copy: copy.start())
-
-    def receive(brick, *kinds):
-        apply(incoming(brick, kinds), lambda copy: copy.wait_recv())
+            if brick != mine:
+                pairs += [(comes, rows_of(brick, route, part)) for part in parts]
+            elif route.half:
+                pairs += [(comes, rows_of(brick, route, None))]
+            if sides:
+                pairs += [
+                    (jnp.logical_and(comes, has_left), cols_of(brick, route)),
+                    (jnp.logical_and(comes, has_right), ends_of(brick, route)),
+                ]
+        apply(pairs, lambda copy: copy.wait_recv())
 
     def close():
-        apply(outgoing(True, ("early", "cols", "ends")), lambda copy: copy.wait_send())
-        apply(outgoing(False, ("early", "late", "cols", "ends")), lambda copy: copy.wait_send())
-
-    return send, receive, close
-
-
-def partners_of(dims, here):
+        for route in routes:
+            apply(rows_out(route), lambda copy: copy.wait_send())
+        apply(ends_sent() + cols_sent(False), lambda copy: copy.wait_send())
+
+    return send_first, send_rest, receive, close
+
+
+def partners_of(dims, here, over):
     ny, nx = dims[:2]
     z, y, x = here
-    cross = 2 * z - 1
-    for side, step in ((z, -1), (z, 0), (z, 1), (1 - z, 0), (1 - z, cross)):
-        for over in (-1, 0, 1):
-            if side is z and isinstance(step, int) and step == 0 and over == 0:
-                continue
-            there = jnp.logical_and(
-                jnp.logical_and(y + step >= 0, y + step < ny),
-                jnp.logical_and(x + over >= 0, x + over < nx),
-            )
-            yield there, (side, y + step, x + over)
+    steps = [(z, over, 0), (1 - z, z if over > 0 else z - 1, 0)]
+    steps += [
+        (side, step, over)
+        for side, step in ((z, -1), (z, 0), (z, 1), (1 - z, 0), (1 - z, 2 * z - 1))
+    ]
+    for side, step, across in steps:
+        yield inside_of(dims, y + step, x + across), (side, y + step, x + across)
+
+
+def inside_of(dims, y, x):
+    ny, nx = dims[:2]
+    return jnp.logical_and(
+        jnp.logical_and(y >= 0, y < ny), jnp.logical_and(x >= 0, x < nx)
+    )
+
+
+def answers_of(dims, here):
+    z, y, x = here
+    own = z == 0
+    yield jnp.logical_and(own, y > 0), (z, y - 1, x), BELOW
+    yield jnp.logical_and(own, y > 0), (1 - z, y - 1, x), BELOW
+    yield jnp.logical_not(own), (1 - z, y, x), FACING
+    for side, kind in ((z, RIGHT), (1 - z, ACROSS)):
+        for step in (0, 2 * z - 1):
+            yield inside_of(dims, y + step, x - 1), (side, y + step, x - 1), kind
 
 
 def render(
     dims, light_in, palette_in, rate_in, shear_in, offset_in, order_in, p_ref, out_ref,
     light, palette, rate, shear, offset, order, tile_ref, m_ref, own_ref, cols_in, ends_in,
-    cols_out, ends_out, h_ref, r_ref, dm, dh, back, sends, arrivals, local_sems, table_sems,
+    cols_out, ends_out, h_ref, r_ref, dm, dh, back, sends, arrivals, ready, local_sems, table_sems,
 ):
     ny, nx, bz, rows = dims
     strip = rows // 2
@@ -327,19 +374,20 @@
             def _():
                 act(mine)
 
-    count = 0
-    for there, who in partners_of(dims, (z, y, x)):
+    for there, who in partners_of(dims, (z, y, x), 1):
 
         @pl.when(there)
         def _():
             pl.semaphore_signal(barrier, inc=1, device_id=who, device_id_type=MESH)
 
+    count = 0
+    for there, _ in partners_of(dims, (z, y, x), -1):
         count = count + there.astype(jnp.int32)
 
     steps = [
         exchange(
             dims, mine, (z, y, x), p_ref, m_ref, cols_out, cols_in, ends_out, ends_in,
-            sends, arrivals,
+            sends, arrivals, ready,
         )
         for mine in range(2)
     ]
@@ -356,6 +404,19 @@
     sided(lambda mine: local_slab(mine).start())
     for copy in tables:
         copy.start()
+
+    @pl.when(count > 0)
+    def _():
+        pl.semaphore_wait(barrier, count)
+
+    for there, who, kind in answers_of(dims, (z, y, x)):
+
+        @pl.when(there)
+        def _():
+            pl.semaphore_signal(ready.at[kind], inc=1, device_id=who, device_id_type=MESH)
+
+
+    sided(lambda mine: steps[mine][0]())
 
     empty = jnp.zeros((tall, LANES), jnp.float32)
     for ref in (m_ref, h_ref):
@@ -453,26 +514,22 @@
                     ends_in[brick, route.half], LANES - 1 - t * bz
                 )
 
-    pl.semaphore_wait(barrier, count)
-
     def opening(mine):
-        send, receive, close = steps[mine]
-        send(False, "early", "cols", "ends")
-        send(True, "early", "cols", "ends")
+        _, send_rest, receive, _ = steps[mine]
+        send_rest()
         local_slab(mine).wait()
-        receive(mine, "early", "cols", "ends")
-        send(False, "late")
+        receive(mine, (), True)
         own_ref[...] = m_ref[1 + mine * bz : 1 + (mine + 1) * bz]
         unpack(mine, mine)
 
     def middle(mine):
-        send, receive, close = steps[mine]
-        receive(1 - mine, "early", "cols", "ends")
+        receive = steps[mine][2]
+        receive(1 - mine, range(PARTS - 1), True)
         unpack(mine, 1 - mine)
 
     def ending(mine):
-        send, receive, close = steps[mine]
-        receive(1 - mine, "late")
+        receive = steps[mine][2]
+        receive(1 - mine, (PARTS - 1,), False)
 
     sided(opening)
     for copy in tables:
@@ -546,7 +603,7 @@
             act(step // per_view, (step % per_view) * tile)
             return carry
 
-        lax.fori_loop(0, VIEWS * per_view, one, 0)
+        lax.fori_loop(0, VIEWS * per_view, one, 0, unroll=VIEWS * per_view)
 
     def own_layer(w, top):
         at = pl.ds(top, tile)
@@ -579,7 +636,7 @@
     sided(ending)
     each((1 - z) * (bz + 1), (1 - z) * (bz + 1) + bz - 1)
     views(other_layer)
-    sided(lambda mine: steps[mine][2]())
+    sided(lambda mine: steps[mine][3]())
 
 
 def two_bricks(mesh, pressure, light, palette, rate, shear, offset, order):
@@ -621,6 +678,7 @@
             pltpu.VMEM((VIEWS, 4, strip, LANES), f32),
             pltpu.SemaphoreType.DMA((SLOTS,)),
             pltpu.SemaphoreType.DMA((SLOTS,)),
+            pltpu.SemaphoreType.REGULAR((4,)),
             pltpu.SemaphoreType.DMA((2,)),
             pltpu.SemaphoreType.DMA((len(tables),)),
         ],

time: 15.2 us -> 13.7 us (0.901)
  the two profiles are of different devices: /device:TPU:19 before, /device:TPU:12 now
where the time goes in v2:
time: 13.7 us; the launch traced here: 13.6 us
  Pallas kernels  12.8 us (93%)
  local copies, waits for them, and re-layouts  0.8 us (6%)
    pallas_call x1, Pallas kernels, two_bricks(): pl.pallas_call(functools.partial(render, dims), out_shape=jax.ShapeDtypeS...  12.8 us
    unnamed x1, local copies, waits for them, and re-layouts  0.8 us

profile of v2, /device:TPU:12, one launch (start us, length us, event | category | flops | bytes accessed | tf_op | source)
XLA Modules:
  0.0 13.6 jit_solution(9949334944126069699)
XLA Ops:
  0.0 12.8 %render.1 = f32[4,4,64,128]{3,2,1,0:T(8,128)S(1)} custom-call(f32[4,3]{1,0:T(4,128)} %light_in.1, f32[2,3]{1,0:T(2,128)} %bitcast.10, f32[4]{0:T(128)} %rate_in.1, s32[4,2,8]{2,1,0:T(2,128)} %bitcast.8, s32[2,2,4]{2,1,0:T(2,128)} %bitcast.9, s32[2,4]{1,0:T(2,128)} %bitcast.11, f32[4,128,128]{2,1,0:T(8,128)} %p_ref.1), custom_call_target="tpu_custom_call" | custom-call | tf_op jit(solution)/shard_map/render/pallas_call | solution.py:660
  12.8 0.8 %copy.10 = f32[4,4,1,64,128]{4,3,2,1,0:T(8,128)} copy(f32[4,4,1,64,128]{4,3,2,1,0:T(8,128)S(1)} %bitcast.7) | data formatting | bytes 1048576

commit v3 on v2

--- a/solution.py
+++ b/solution.py
@@ -175,9 +175,9 @@
     return routes, sent, max(routes[0].size + routes[1].size, routes[2].size + routes[3].size)
 
 
-MAIN, EDGE, BESIDE, COLS, ENDS, SLOTS = 0, 3, 6, 7, 11, 15
-PARTS = 3
-FACING, BELOW, RIGHT, ACROSS = range(4)
+MAIN, EDGE, BESIDE, COLS, ENDS, SLOTS = 0, 2, 4, 5, 9, 13
+PARTS = 2
+BELOW, RIGHT, ACROSS = range(3)
 
 
 def exchange(
@@ -189,33 +189,33 @@
     has_up, has_down = y > 0, y < ny - 1
     routes = routes_of(dims)[0]
 
-    def remote(src, dst, sent, arrival, who):
+    def remote(src, dst, arrival, who):
         return pltpu.make_async_remote_copy(
             src_ref=src,
             dst_ref=dst,
-            send_sem=sends.at[sent],
+            send_sem=sends,
             recv_sem=arrivals.at[arrival],
             device_id=who,
             device_id_type=MESH,
         )
 
     def rows_of(brick, route, part):
-        start = 0 if part is None else part
-        count = bz if part is None else (bz - part if part == PARTS - 1 else 1)
+        start = part * (bz // PARTS) if part else 0
+        count = bz if part is None else bz // PARTS
         if part is not None and brick == 0:
             start = bz - start - count
         slot = BESIDE if part is None else (EDGE if route.half else MAIN) + part
         return remote(
             p_ref.at[pl.ds(start, count), route.rows],
             m_ref.at[pl.ds(1 + brick * bz + start, count), route.slab],
-            slot, slot, (route.side, y + route.step, x),
+            slot, (route.side, y + route.step, x),
         )
 
     def cols_of(brick, route):
         return remote(
             cols_out.at[pl.ds(route.sent, route.size)],
             cols_in.at[brick, pl.ds(route.base, route.size)],
-            COLS + 2 * route.side + route.half, COLS + 2 * brick + route.half,
+            COLS + 2 * brick + route.half,
             (route.side, y + route.step, x + 1),
         )
 
@@ -223,14 +223,15 @@
         return remote(
             ends_out,
             ends_in.at[brick, route.half],
-            ENDS + 2 * route.side + route.half, ENDS + 2 * brick + route.half,
+            ENDS + 2 * brick + route.half,
             (route.side, y + route.step, x - 1),
         )
 
-    def rows_out(route):
+    def rows_out(route, late=False):
         there = route.there(y, ny)
         if route.side != mine:
-            return [(there, rows_of(mine, route, part)) for part in range(PARTS)]
+            parts = (PARTS - 1,) if late else range(PARTS - 1)
+            return [(there, rows_of(mine, route, part)) for part in parts]
         return [(there, rows_of(mine, route, None))] if route.half else []
 
     def cols_sent(same):
@@ -265,6 +266,7 @@
 
     def send_first():
         if mine == 0:
+            start(rows_out(mains))
             start(rows_out(halos))
         else:
             start(rows_out(mains))
@@ -272,8 +274,6 @@
 
     def send_rest():
         if mine == 0:
-            heard(FACING, y >= 0, 1)
-            start(rows_out(mains))
             start(ends_sent())
             heard(BELOW, has_down, 1)
             start(rows_out(own_halo))
@@ -284,8 +284,8 @@
         heard(RIGHT, has_right, next_ones[mine])
         start(cols_sent(True))
         heard(ACROSS, has_right, next_ones[1 - mine])
-        apply(cols_sent(True), lambda copy: copy.wait_send())
         start(cols_sent(False))
+        start(rows_out(mains, True) + rows_out(halos, True))
 
     def receive(brick, parts, sides):
         pairs = []
@@ -305,9 +305,10 @@
         apply(pairs, lambda copy: copy.wait_recv())
 
     def close():
-        for route in routes:
-            apply(rows_out(route), lambda copy: copy.wait_send())
-        apply(ends_sent() + cols_sent(False), lambda copy: copy.wait_send())
+        for late in (False, True):
+            apply(rows_out(mains, late) + rows_out(halos, late), lambda copy: copy.wait_send())
+        apply(rows_out(own_halo), lambda copy: copy.wait_send())
+        apply(ends_sent() + cols_sent(True) + cols_sent(False), lambda copy: copy.wait_send())
 
     return send_first, send_rest, receive, close
 
@@ -315,7 +316,9 @@
 def partners_of(dims, here, over):
     ny, nx = dims[:2]
     z, y, x = here
-    steps = [(z, over, 0), (1 - z, z if over > 0 else z - 1, 0)]
+    steps = [(z, over, 0), (1 - z, 0, 0)]
+    diagonal = z == 1 if over > 0 else z == 0
+    yield jnp.logical_and(diagonal, inside_of(dims, y + over, x)), (1 - z, y + over, x)
     steps += [
         (side, step, over)
         for side, step in ((z, -1), (z, 0), (z, 1), (1 - z, 0), (1 - z, 2 * z - 1))
@@ -336,7 +339,6 @@
     own = z == 0
     yield jnp.logical_and(own, y > 0), (z, y - 1, x), BELOW
     yield jnp.logical_and(own, y > 0), (1 - z, y - 1, x), BELOW
-    yield jnp.logical_not(own), (1 - z, y, x), FACING
     for side, kind in ((z, RIGHT), (1 - z, ACROSS)):
         for step in (0, 2 * z - 1):
             yield inside_of(dims, y + step, x - 1), (side, y + step, x - 1), kind
@@ -345,7 +347,7 @@
 def render(
     dims, light_in, palette_in, rate_in, shear_in, offset_in, order_in, p_ref, out_ref,
     light, palette, rate, shear, offset, order, tile_ref, m_ref, own_ref, cols_in, ends_in,
-    cols_out, ends_out, h_ref, r_ref, dm, dh, back, sends, arrivals, ready, local_sems, table_sems,
+    cols_out, ends_out, h_ref, r_ref, dm, dh, back, sends, arrivals, ready, local_sems, table_sem,
 ):
     ny, nx, bz, rows = dims
     strip = rows // 2
@@ -357,12 +359,10 @@
     routes = routes_of(dims)[0]
 
     tables = [
-        pltpu.make_async_copy(source, target, table_sems.at[i])
-        for i, (source, target) in enumerate(
-            (
-                (light_in, light), (palette_in, palette), (rate_in, rate),
-                (shear_in, shear), (offset_in, offset), (order_in, order),
-            )
+        pltpu.make_async_copy(source, target, table_sem)
+        for source, target in (
+            (light_in, light), (palette_in, palette), (rate_in, rate),
+            (shear_in, shear), (offset_in, offset), (order_in, order),
         )
     ]
     barrier = pltpu.get_barrier_semaphore()
@@ -676,11 +676,11 @@
             pltpu.VMEM((VIEWS, depth, HALO + strip, LANES), f32),
             pltpu.VMEM((VIEWS, depth, HALO + strip, LANES), f32),
             pltpu.VMEM((VIEWS, 4, strip, LANES), f32),
+            pltpu.SemaphoreType.DMA,
             pltpu.SemaphoreType.DMA((SLOTS,)),
-            pltpu.SemaphoreType.DMA((SLOTS,)),
-            pltpu.SemaphoreType.REGULAR((4,)),
+            pltpu.SemaphoreType.REGULAR((3,)),
             pltpu.SemaphoreType.DMA((2,)),
-            pltpu.SemaphoreType.DMA((len(tables),)),
+            pltpu.SemaphoreType.DMA,
         ],
         compiler_params=pltpu.CompilerParams(collective_id=0, has_side_effects=True, vmem_limit_bytes=12 << 20),
         name="render",

time: 13.7 us -> 13.3 us (0.971)
  the two profiles are of different devices: /device:TPU:12 before, /device:TPU:11 now
where the time goes in v3:
time: 13.3 us; the launch traced here: 13.2 us
  Pallas kernels  12.4 us (93%)
  local copies, waits for them, and re-layouts  0.8 us (6%)
    pallas_call x1, Pallas kernels, two_bricks(): pl.pallas_call(functools.partial(render, dims), out_shape=jax.ShapeDtypeS...  12.4 us
    unnamed x1, local copies, waits for them, and re-layouts  0.8 us

profile of v3, /device:TPU:11, one launch (start us, length us, event | category | flops | bytes accessed | tf_op | source)
XLA Modules:
  0.0 13.2 jit_solution(3964107041122885774)
XLA Ops:
  0.0 12.4 %render.1 = f32[4,4,64,128]{3,2,1,0:T(8,128)S(1)} custom-call(f32[4,3]{1,0:T(4,128)} %light_in.1, f32[2,3]{1,0:T(2,128)} %bitcast.10, f32[4]{0:T(128)} %rate_in.1, s32[4,2,8]{2,1,0:T(2,128)} %bitcast.8, s32[2,2,4]{2,1,0:T(2,128)} %bitcast.9, s32[2,4]{1,0:T(2,128)} %bitcast.11, f32[4,128,128]{2,1,0:T(8,128)} %p_ref.1), custom_call_target="tpu_custom_call" | custom-call | tf_op jit(solution)/shard_map/render/pallas_call | solution.py:660
  12.4 0.8 %copy.10 = f32[4,4,1,64,128]{4,3,2,1,0:T(8,128)} copy(f32[4,4,1,64,128]{4,3,2,1,0:T(8,128)S(1)} %bitcast.7) | data formatting | bytes 1048576

commit v4 on v3

--- a/solution.py
+++ b/solution.py
@@ -175,8 +175,8 @@
     return routes, sent, max(routes[0].size + routes[1].size, routes[2].size + routes[3].size)
 
 
-MAIN, EDGE, BESIDE, COLS, ENDS, SLOTS = 0, 2, 4, 5, 9, 13
-PARTS = 2
+MAIN, EDGE, BESIDE, COLS, ENDS, SLOTS = 0, 3, 6, 7, 11, 15
+PARTS = 3
 BELOW, RIGHT, ACROSS = range(3)
 
 
@@ -200,8 +200,9 @@
         )
 
     def rows_of(brick, route, part):
-        start = part * (bz // PARTS) if part else 0
-        count = bz if part is None else bz // PARTS
+        first = bz - PARTS + 1
+        start = first + part - 1 if part else 0
+        count = bz if part is None else 1 if part else first
         if part is not None and brick == 0:
             start = bz - start - count
         slot = BESIDE if part is None else (EDGE if route.half else MAIN) + part
@@ -227,11 +228,10 @@
             (route.side, y + route.step, x - 1),
         )
 
-    def rows_out(route, late=False):
+    def rows_out(route, part=0):
         there = route.there(y, ny)
         if route.side != mine:
-            parts = (PARTS - 1,) if late else range(PARTS - 1)
-            return [(there, rows_of(mine, route, part)) for part in parts]
+            return [(there, rows_of(mine, route, part))]
         return [(there, rows_of(mine, route, None))] if route.half else []
 
     def cols_sent(same):
@@ -285,7 +285,10 @@
         start(cols_sent(True))
         heard(ACROSS, has_right, next_ones[1 - mine])
         start(cols_sent(False))
-        start(rows_out(mains, True) + rows_out(halos, True))
+        start(rows_out(mains, 1) + rows_out(halos, 1))
+
+    def send_last():
+        start(rows_out(mains, 2) + rows_out(halos, 2))
 
     def receive(brick, parts, sides):
         pairs = []
@@ -305,12 +308,12 @@
         apply(pairs, lambda copy: copy.wait_recv())
 
     def close():
-        for late in (False, True):
-            apply(rows_out(mains, late) + rows_out(halos, late), lambda copy: copy.wait_send())
+        for part in range(PARTS):
+            apply(rows_out(mains, part) + rows_out(halos, part), lambda copy: copy.wait_send())
         apply(rows_out(own_halo), lambda copy: copy.wait_send())
         apply(ends_sent() + cols_sent(True) + cols_sent(False), lambda copy: copy.wait_send())
 
-    return send_first, send_rest, receive, close
+    return send_first, send_rest, send_last, receive, close
 
 
 def partners_of(dims, here, over):
@@ -515,21 +518,22 @@
                 )
 
     def opening(mine):
-        _, send_rest, receive, _ = steps[mine]
+        _, send_rest, send_last, receive, _ = steps[mine]
         send_rest()
         local_slab(mine).wait()
         receive(mine, (), True)
+        send_last()
         own_ref[...] = m_ref[1 + mine * bz : 1 + (mine + 1) * bz]
         unpack(mine, mine)
 
     def middle(mine):
-        receive = steps[mine][2]
-        receive(1 - mine, range(PARTS - 1), True)
+        receive = steps[mine][3]
+        receive(1 - mine, (0,), True)
         unpack(mine, 1 - mine)
 
-    def ending(mine):
-        receive = steps[mine][2]
-        receive(1 - mine, (PARTS - 1,), False)
+    def ending(mine, part):
+        receive = steps[mine][3]
+        receive(1 - mine, (part,), False)
 
     sided(opening)
     for copy in tables:
@@ -633,10 +637,12 @@
     sided(middle)
     each(bz - 1, bz + 1)
     views(own_layer)
-    sided(ending)
-    each((1 - z) * (bz + 1), (1 - z) * (bz + 1) + bz - 1)
+    sided(lambda mine: ending(mine, 1))
+    each(bz + 1 - 3 * z, bz + 2 - 3 * z)
+    sided(lambda mine: ending(mine, 2))
+    each((1 - z) * (depth - 2), (1 - z) * (depth - 2) + 2)
     views(other_layer)
-    sided(lambda mine: steps[mine][3]())
+    sided(lambda mine: steps[mine][4]())
 
 
 def two_bricks(mesh, pressure, light, palette, rate, shear, offset, order):

time: 13.3 us -> 13.1 us (0.985)
  Pallas kernels: 12.4 us -> 12.2 us
    pallas_call x1, Pallas kernels: 12.4 us -> 12.2 us  [two_bricks(): pl.pallas_call(functools.partial(render, dims), out_shape=jax.ShapeDtypeS...]
where the time goes in v4:
time: 13.1 us; the launch traced here: 13 us
  Pallas kernels  12.2 us (93%)
  local copies, waits for them, and re-layouts  0.8 us (6%)
    pallas_call x1, Pallas kernels, two_bricks(): pl.pallas_call(functools.partial(render, dims), out_shape=jax.ShapeDtypeS...  12.2 us
    unnamed x1, local copies, waits for them, and re-layouts  0.8 us

profile of v4, /device:TPU:11, one launch (start us, length us, event | category | flops | bytes accessed | tf_op | source)
XLA Modules:
  0.0 13.0 jit_solution(832559026201463261)
XLA Ops:
  0.0 12.2 %render.1 = f32[4,4,64,128]{3,2,1,0:T(8,128)S(1)} custom-call(f32[4,3]{1,0:T(4,128)} %light_in.1, f32[2,3]{1,0:T(2,128)} %bitcast.10, f32[4]{0:T(128)} %rate_in.1, s32[4,2,8]{2,1,0:T(2,128)} %bitcast.8, s32[2,2,4]{2,1,0:T(2,128)} %bitcast.9, s32[2,4]{1,0:T(2,128)} %bitcast.11, f32[4,128,128]{2,1,0:T(8,128)} %p_ref.1), custom_call_target="tpu_custom_call" | custom-call | tf_op jit(solution)/shard_map/render/pallas_call | solution.py:666
  12.2 0.8 %copy.10 = f32[4,4,1,64,128]{4,3,2,1,0:T(8,128)} copy(f32[4,4,1,64,128]{4,3,2,1,0:T(8,128)S(1)} %bitcast.7) | data formatting | bytes 1048576

commit v5 on v4

--- a/solution.py
+++ b/solution.py
@@ -177,7 +177,7 @@
 
 MAIN, EDGE, BESIDE, COLS, ENDS, SLOTS = 0, 3, 6, 7, 11, 15
 PARTS = 3
-BELOW, RIGHT, ACROSS = range(3)
+BELOW, RIGHT, ACROSS, FACING = range(4)
 
 
 def exchange(
@@ -262,28 +262,28 @@
     mains, own_halo, halos = (
         (routes[2], routes[1], routes[3]) if mine == 0 else (routes[0], routes[3], routes[1])
     )
-    next_ones = [1 + there.astype(jnp.int32) for there in (has_down, has_up)]
+    also_down = jnp.logical_and(has_right, has_down)
 
     def send_first():
-        if mine == 0:
-            start(rows_out(mains))
-            start(rows_out(halos))
-        else:
-            start(rows_out(mains))
+        start(rows_out(mains))
+        if mine == 1:
             start(rows_out(own_halo))
 
     def send_rest():
         if mine == 0:
-            start(ends_sent())
+            heard(FACING, y >= 0, 1)
+            start(rows_out(halos))
             heard(BELOW, has_down, 1)
-            start(rows_out(own_halo))
+            start(rows_out(own_halo) + ends_sent())
+            heard(RIGHT, has_right, 1 + has_down.astype(jnp.int32))
+            start(cols_sent(True))
+            heard(ACROSS, has_right, 1)
         else:
-            start(ends_sent())
             heard(BELOW, has_down, 1)
-            start(rows_out(halos))
-        heard(RIGHT, has_right, next_ones[mine])
-        start(cols_sent(True))
-        heard(ACROSS, has_right, next_ones[1 - mine])
+            start(rows_out(halos) + ends_sent())
+            heard(RIGHT, has_right, 1)
+            start(cols_sent(True))
+            heard(ACROSS, also_down, 1)
         start(cols_sent(False))
         start(rows_out(mains, 1) + rows_out(halos, 1))
 
@@ -316,35 +316,17 @@
     return send_first, send_rest, send_last, receive, close
 
 
-def partners_of(dims, here, over):
-    ny, nx = dims[:2]
-    z, y, x = here
-    steps = [(z, over, 0), (1 - z, 0, 0)]
-    diagonal = z == 1 if over > 0 else z == 0
-    yield jnp.logical_and(diagonal, inside_of(dims, y + over, x)), (1 - z, y + over, x)
-    steps += [
-        (side, step, over)
-        for side, step in ((z, -1), (z, 0), (z, 1), (1 - z, 0), (1 - z, 2 * z - 1))
-    ]
-    for side, step, across in steps:
-        yield inside_of(dims, y + step, x + across), (side, y + step, x + across)
-
-
-def inside_of(dims, y, x):
-    ny, nx = dims[:2]
-    return jnp.logical_and(
-        jnp.logical_and(y >= 0, y < ny), jnp.logical_and(x >= 0, x < nx)
-    )
-
-
 def answers_of(dims, here):
     z, y, x = here
-    own = z == 0
-    yield jnp.logical_and(own, y > 0), (z, y - 1, x), BELOW
-    yield jnp.logical_and(own, y > 0), (1 - z, y - 1, x), BELOW
-    for side, kind in ((z, RIGHT), (1 - z, ACROSS)):
-        for step in (0, 2 * z - 1):
-            yield inside_of(dims, y + step, x - 1), (side, y + step, x - 1), kind
+    up, left, lower = y > 0, x > 0, z == 0
+    both = jnp.logical_and(up, left)
+    upper = jnp.logical_not(lower)
+    yield up, (z, y - 1, x), BELOW
+    yield left, (z, y, x - 1), RIGHT
+    yield jnp.logical_and(both, lower), (z, y - 1, x - 1), RIGHT
+    yield jnp.logical_and(both, upper), (z, y - 1, x - 1), ACROSS
+    yield jnp.logical_and(left, upper), (1 - z, y, x - 1), ACROSS
+    yield upper, (1 - z, y, x), FACING
 
 
 def render(
@@ -377,15 +359,13 @@
             def _():
                 act(mine)
 
-    for there, who in partners_of(dims, (z, y, x), 1):
-
+    def greet(there, who):
         @pl.when(there)
         def _():
             pl.semaphore_signal(barrier, inc=1, device_id=who, device_id_type=MESH)
 
-    count = 0
-    for there, _ in partners_of(dims, (z, y, x), -1):
-        count = count + there.astype(jnp.int32)
+    greet(z >= 0, (1 - z, y, x))
+    greet(y < ny - 1, (z, y + 1, x))
 
     steps = [
         exchange(
@@ -408,10 +388,8 @@
     for copy in tables:
         copy.start()
 
-    @pl.when(count > 0)
-    def _():
-        pl.semaphore_wait(barrier, count)
-
+    pl.semaphore_wait(barrier, 1 + (y > 0).astype(jnp.int32) + (x > 0).astype(jnp.int32))
+    greet(x < nx - 1, (z, y, x + 1))
     for there, who, kind in answers_of(dims, (z, y, x)):
 
         @pl.when(there)
@@ -561,7 +539,7 @@
             ):
                 deep = ref[k + 2, top + 1 : top + 1 + SUB] - ref[k, top + 1 : top + 1 + SUB]
                 down = ref[k + 1, top + 2 : top + 2 + SUB] - ref[k + 1, top : top + SUB]
-                half = 0.5 * lax.rsqrt(0.25 * (deep * deep + down * down + cols * cols) + 1.0)
+                half = lax.rsqrt(deep * deep + down * down + cols * cols + 4.0)
                 deep, down, cols = deep * half, down * half, cols * half
                 for w in range(VIEWS):
                     a, b, c = towards[w]
@@ -684,7 +662,7 @@
             pltpu.VMEM((VIEWS, 4, strip, LANES), f32),
             pltpu.SemaphoreType.DMA,
             pltpu.SemaphoreType.DMA((SLOTS,)),
-            pltpu.SemaphoreType.REGULAR((3,)),
+            pltpu.SemaphoreType.REGULAR((4,)),
             pltpu.SemaphoreType.DMA((2,)),
             pltpu.SemaphoreType.DMA,
         ],

time: 13.1 us -> 14.5 us (1.11)
  the two profiles are of different devices: /device:TPU:11 before, /device:TPU:27 now
where the time goes in v5:
time: 14.5 us; the launch traced here: 14.3 us
  Pallas kernels  13.5 us (93%)
  local copies, waits for them, and re-layouts  0.8 us (6%)
    pallas_call x1, Pallas kernels, two_bricks(): pl.pallas_call(functools.partial(render, dims), out_shape=jax.ShapeDtypeS...  13.5 us
    unnamed x1, local copies, waits for them, and re-layouts  0.8 us

profile of v5, /device:TPU:27, one launch (start us, length us, event | category | flops | bytes accessed | tf_op | source)
XLA Modules:
  0.0 14.3 jit_solution(18113548067116217122)
XLA Ops:
  0.0 13.5 %render.1 = f32[4,4,64,128]{3,2,1,0:T(8,128)S(1)} custom-call(f32[4,3]{1,0:T(4,128)} %light_in.1, f32[2,3]{1,0:T(2,128)} %bitcast.10, f32[4]{0:T(128)} %rate_in.1, s32[4,2,8]{2,1,0:T(2,128)} %bitcast.8, s32[2,2,4]{2,1,0:T(2,128)} %bitcast.9, s32[2,4]{1,0:T(2,128)} %bitcast.11, f32[4,128,128]{2,1,0:T(8,128)} %p_ref.1), custom_call_target="tpu_custom_call" | custom-call | tf_op jit(solution)/shard_map/render/pallas_call | solution.py:644
  13.5 0.8 %copy.10 = f32[4,4,1,64,128]{4,3,2,1,0:T(8,128)} copy(f32[4,4,1,64,128]{4,3,2,1,0:T(8,128)S(1)} %bitcast.7) | data formatting | bytes 1048576

commit v6 on v4

--- a/solution.py
+++ b/solution.py
@@ -135,7 +135,9 @@
     def __init__(self, dims, side, step, start, count, slab, half):
         bz = dims[2]
         self.side, self.step, self.half = side, step, half
-        self.rows, self.slab = pl.ds(start, count), pl.ds(slab, count)
+        self.slab = pl.ds(slab, count)
+        needed = count - SUB + 1 if start == 0 else count
+        self.rows, self.lands = pl.ds(start, needed), pl.ds(slab, needed)
         self.groups = LANES // (SUB * bz)
         self.tiles = range(start // SUB, (start + count) // SUB)
         self.first = slab // SUB
@@ -208,7 +210,7 @@
         slot = BESIDE if part is None else (EDGE if route.half else MAIN) + part
         return remote(
             p_ref.at[pl.ds(start, count), route.rows],
-            m_ref.at[pl.ds(1 + brick * bz + start, count), route.slab],
+            m_ref.at[pl.ds(1 + brick * bz + start, count), route.lands],
             slot, (route.side, y + route.step, x),
         )
 
@@ -398,7 +400,7 @@
     def local_slab(mine):
         route = routes[2 * mine]
         return pltpu.make_async_copy(
-            p_ref.at[:, route.rows], m_ref.at[pl.ds(1 + mine * bz, bz), route.slab],
+            p_ref.at[:, route.rows], m_ref.at[pl.ds(1 + mine * bz, bz), route.lands],
             local_sems.at[1],
         )
 
@@ -561,7 +563,7 @@
             ):
                 deep = ref[k + 2, top + 1 : top + 1 + SUB] - ref[k, top + 1 : top + 1 + SUB]
                 down = ref[k + 1, top + 2 : top + 2 + SUB] - ref[k + 1, top : top + SUB]
-                half = 0.5 * lax.rsqrt(0.25 * (deep * deep + down * down + cols * cols) + 1.0)
+                half = lax.rsqrt(deep * deep + down * down + cols * cols + 4.0)
                 deep, down, cols = deep * half, down * half, cols * half
                 for w in range(VIEWS):
                     a, b, c = towards[w]

time: 13.1 us -> 13.1 us (level)
  no operation moved by 1% of the time
where the time goes in v6:
time: 13.1 us; the launch traced here: 12.9 us
  Pallas kernels  12.1 us (92%)
  local copies, waits for them, and re-layouts  0.8 us (6%)
    pallas_call x1, Pallas kernels, two_bricks(): pl.pallas_call(functools.partial(render, dims), out_shape=jax.ShapeDtypeS...  12.1 us
    unnamed x1, local copies, waits for them, and re-layouts  0.8 us

profile of v6, /device:TPU:11, one launch (start us, length us, event | category | flops | bytes accessed | tf_op | source)
XLA Modules:
  0.0 12.9 jit_solution(14462348216080684726)
XLA Ops:
  0.0 12.1 %render.1 = f32[4,4,64,128]{3,2,1,0:T(8,128)S(1)} custom-call(f32[4,3]{1,0:T(4,128)} %light_in.1, f32[2,3]{1,0:T(2,128)} %bitcast.10, f32[4]{0:T(128)} %rate_in.1, s32[4,2,8]{2,1,0:T(2,128)} %bitcast.8, s32[2,2,4]{2,1,0:T(2,128)} %bitcast.9, s32[2,4]{1,0:T(2,128)} %bitcast.11, f32[4,128,128]{2,1,0:T(8,128)} %p_ref.1), custom_call_target="tpu_custom_call" | custom-call | tf_op jit(solution)/shard_map/render/pallas_call | solution.py:668
  12.2 0.8 %copy.10 = f32[4,4,1,64,128]{4,3,2,1,0:T(8,128)} copy(f32[4,4,1,64,128]{4,3,2,1,0:T(8,128)S(1)} %bitcast.7) | data formatting | bytes 1048576

commit v7 on v6

--- a/solution.py
+++ b/solution.py
@@ -268,8 +268,8 @@
 
     def send_first():
         if mine == 0:
+            start(rows_out(halos))
             start(rows_out(mains))
-            start(rows_out(halos))
         else:
             start(rows_out(mains))
             start(rows_out(own_halo))
@@ -281,16 +281,15 @@
             start(rows_out(own_halo))
         else:
             start(ends_sent())
+        heard(RIGHT, has_right, next_ones[mine])
+        start(cols_sent(True))
+        if mine == 1:
             heard(BELOW, has_down, 1)
             start(rows_out(halos))
-        heard(RIGHT, has_right, next_ones[mine])
-        start(cols_sent(True))
         heard(ACROSS, has_right, next_ones[1 - mine])
         start(cols_sent(False))
-        start(rows_out(mains, 1) + rows_out(halos, 1))
-
-    def send_last():
-        start(rows_out(mains, 2) + rows_out(halos, 2))
+        for part in range(1, PARTS):
+            start(rows_out(halos, part) + rows_out(mains, part))
 
     def receive(brick, parts, sides):
         pairs = []
@@ -315,7 +314,7 @@
         apply(rows_out(own_halo), lambda copy: copy.wait_send())
         apply(ends_sent() + cols_sent(True) + cols_sent(False), lambda copy: copy.wait_send())
 
-    return send_first, send_rest, send_last, receive, close
+    return send_first, send_rest, receive, close
 
 
 def partners_of(dims, here, over):
@@ -520,21 +519,20 @@
                 )
 
     def opening(mine):
-        _, send_rest, send_last, receive, _ = steps[mine]
+        _, send_rest, receive, _ = steps[mine]
         send_rest()
         local_slab(mine).wait()
         receive(mine, (), True)
-        send_last()
         own_ref[...] = m_ref[1 + mine * bz : 1 + (mine + 1) * bz]
         unpack(mine, mine)
 
     def middle(mine):
-        receive = steps[mine][3]
+        receive = steps[mine][2]
         receive(1 - mine, (0,), True)
         unpack(mine, 1 - mine)
 
     def ending(mine, part):
-        receive = steps[mine][3]
+        receive = steps[mine][2]
         receive(1 - mine, (part,), False)
 
     sided(opening)
@@ -644,7 +642,7 @@
     sided(lambda mine: ending(mine, 2))
     each((1 - z) * (depth - 2), (1 - z) * (depth - 2) + 2)
     views(other_layer)
-    sided(lambda mine: steps[mine][4]())
+    sided(lambda mine: steps[mine][3]())
 
 
 def two_bricks(mesh, pressure, light, palette, rate, shear, offset, order):

time: 13.1 us -> 12.5 us (0.954)
  the two profiles are of different devices: /device:TPU:11 before, /device:TPU:9 now
where the time goes in v7:
time: 12.5 us; the launch traced here: 12.3 us
  Pallas kernels  11.5 us (92%)
  local copies, waits for them, and re-layouts  0.8 us (6%)
    pallas_call x1, Pallas kernels, two_bricks(): pl.pallas_call(functools.partial(render, dims), out_shape=jax.ShapeDtypeS...  11.5 us
    unnamed x1, local copies, waits for them, and re-layouts  0.8 us

profile of v7, /device:TPU:9, one launch (start us, length us, event | category | flops | bytes accessed | tf_op | source)
XLA Modules:
  0.0 12.3 jit_solution(7072299605194785543)
XLA Ops:
  0.0 11.5 %render.1 = f32[4,4,64,128]{3,2,1,0:T(8,128)S(1)} custom-call(f32[4,3]{1,0:T(4,128)} %light_in.1, f32[2,3]{1,0:T(2,128)} %bitcast.10, f32[4]{0:T(128)} %rate_in.1, s32[4,2,8]{2,1,0:T(2,128)} %bitcast.8, s32[2,2,4]{2,1,0:T(2,128)} %bitcast.9, s32[2,4]{1,0:T(2,128)} %bitcast.11, f32[4,128,128]{2,1,0:T(8,128)} %p_ref.1), custom_call_target="tpu_custom_call" | custom-call | tf_op jit(solution)/shard_map/render/pallas_call | solution.py:666
  11.5 0.8 %copy.10 = f32[4,4,1,64,128]{4,3,2,1,0:T(8,128)} copy(f32[4,4,1,64,128]{4,3,2,1,0:T(8,128)S(1)} %bitcast.7) | data formatting | bytes 1048576

commit v8 on v7

--- a/solution.py
+++ b/solution.py
@@ -286,10 +286,10 @@
         if mine == 1:
             heard(BELOW, has_down, 1)
             start(rows_out(halos))
+        start(rows_out(halos, 1) + rows_out(mains, 1))
         heard(ACROSS, has_right, next_ones[1 - mine])
         start(cols_sent(False))
-        for part in range(1, PARTS):
-            start(rows_out(halos, part) + rows_out(mains, part))
+        start(rows_out(halos, 2) + rows_out(mains, 2))
 
     def receive(brick, parts, sides):
         pairs = []
@@ -635,12 +635,14 @@
 
     each(z * (bz + 1), z * (bz + 1) + bz - 1)
     sided(middle)
-    each(bz - 1, bz + 1)
+    for k in range(2):
+        slopes(bz - 1 + k, 0)
     views(own_layer)
     sided(lambda mine: ending(mine, 1))
     each(bz + 1 - 3 * z, bz + 2 - 3 * z)
     sided(lambda mine: ending(mine, 2))
-    each((1 - z) * (depth - 2), (1 - z) * (depth - 2) + 2)
+    for k in range(2):
+        slopes((1 - z) * (depth - 2) + k, 0)
     views(other_layer)
     sided(lambda mine: steps[mine][3]())
 

time: 12.5 us -> 12.4 us (level)
  no operation moved by 1% of the time
where the time goes in v8:
time: 12.4 us; the launch traced here: 12.3 us
  Pallas kernels  11.5 us (93%)
  local copies, waits for them, and re-layouts  0.8 us (6%)
    pallas_call x1, Pallas kernels, two_bricks(): pl.pallas_call(functools.partial(render, dims), out_shape=jax.ShapeDtypeS...  11.5 us
    unnamed x1, local copies, waits for them, and re-layouts  0.8 us

profile of v8, /device:TPU:9, one launch (start us, length us, event | category | flops | bytes accessed | tf_op | source)
XLA Modules:
  0.0 12.3 jit_solution(13406793645572908992)
XLA Ops:
  0.0 11.5 %render.1 = f32[4,4,64,128]{3,2,1,0:T(8,128)S(1)} custom-call(f32[4,3]{1,0:T(4,128)} %light_in.1, f32[2,3]{1,0:T(2,128)} %bitcast.10, f32[4]{0:T(128)} %rate_in.1, s32[4,2,8]{2,1,0:T(2,128)} %bitcast.8, s32[2,2,4]{2,1,0:T(2,128)} %bitcast.9, s32[2,4]{1,0:T(2,128)} %bitcast.11, f32[4,128,128]{2,1,0:T(8,128)} %p_ref.1), custom_call_target="tpu_custom_call" | custom-call | tf_op jit(solution)/shard_map/render/pallas_call | solution.py:668
  11.5 0.8 %copy.10 = f32[4,4,1,64,128]{4,3,2,1,0:T(8,128)} copy(f32[4,4,1,64,128]{4,3,2,1,0:T(8,128)S(1)} %bitcast.7) | data formatting | bytes 1048576

commit v9 on v8

--- a/solution.py
+++ b/solution.py
@@ -350,7 +350,7 @@
 
 def render(
     dims, light_in, palette_in, rate_in, shear_in, offset_in, order_in, p_ref, out_ref,
-    light, palette, rate, shear, offset, order, tile_ref, m_ref, own_ref, cols_in, ends_in,
+    light, palette, rate, shear, offset, order, tile_ref, m_ref, own_ref, near_ref, cols_in, ends_in,
     cols_out, ends_out, h_ref, r_ref, dm, dh, back, sends, arrivals, ready, local_sems, table_sem,
 ):
     ny, nx, bz, rows = dims
@@ -529,6 +529,7 @@
     def middle(mine):
         receive = steps[mine][2]
         receive(1 - mine, (0,), True)
+        near_ref[...] = m_ref[(bz if mine == 0 else 2) + 1 : (depth - 2 if mine == 0 else bz) + 1]
         unpack(mine, 1 - mine)
 
     def ending(mine, part):
@@ -577,14 +578,14 @@
     bias = [0.5 * palette[0, c] for c in range(3)]
     gain = [0.5 * palette[1, c] for c in range(3)]
 
-    def march(w, top, brick, cells, start, colors, through):
+    def march(w, top, brick, first_k, count, cells, start, colors, through):
         ambient = jnp.zeros((tile, LANES), jnp.float32)
         rate2 = rate[w] * (-math.log2(math.e))
         off_r, off_c = offset[brick, 0, w], offset[brick, 1, w]
         inside = jnp.logical_and(rows_at >= off_r - base_row - top, lanes >= off_c - base_col)
         fall = jnp.where(inside, rate2, 0.0)
-        for j in range(bz):
-            k = brick * bz + j
+        for j in range(count):
+            k = first_k + j
             sr = off_r + shear[w, 0, k]
             sc = off_c + shear[w, 1, k]
             at = HALO + top - sr
@@ -609,21 +610,41 @@
 
         lax.fori_loop(0, VIEWS * per_view, one, 0, unroll=VIEWS * per_view)
 
+    zero = jnp.zeros((tile, LANES), jnp.float32)
+    early = bz - 2
+    near, far = bz - early * z, (depth - 2) * (1 - z)
+
     def own_layer(w, top):
         at = pl.ds(top, tile)
-        zero = jnp.zeros((tile, LANES), jnp.float32)
-        colors, through = march(w, top, z, own_ref, 0, [zero] * 3, zero + 1.0)
-        ahead = order[0, w] == z
+        colors, through = march(w, top, z, z * bz, bz, own_ref, 0, [zero] * 3, zero + 1.0)
         for c in range(3):
-            out_ref[w, c, at] = jnp.where(ahead, colors[c], 0.0)
-            back[w, c, at] = jnp.where(ahead, 0.0, colors[c])
-        out_ref[w, 3, at] = jnp.where(ahead, through, 1.0)
-        back[w, 3, at] = jnp.where(ahead, 1.0, through)
-
-    def other_layer(w, top):
+            back[w, c, at] = colors[c]
+        back[w, 3, at] = through
+
+    def near_layer(w, top):
         at = pl.ds(top, tile)
         colors, through = march(
-            w, top, 1 - z, m_ref, 1 + (1 - z) * bz, [out_ref[w, c, at] for c in range(3)],
+            w, top, 1 - z, near, early, near_ref, 0, [zero] * 3, zero + 1.0
+        )
+        own_first, near_first = order[0, w] == z, z == 0
+        own_through = back[w, 3, at]
+        ahead = jnp.where(own_first, own_through, 1.0)
+        after = jnp.where(near_first, 1.0, through)
+        for c in range(3):
+            own_color = back[w, c, at]
+            out_ref[w, c, at] = jnp.where(own_first, own_color, 0.0) + jnp.where(
+                near_first, ahead * colors[c], 0.0
+            )
+            back[w, c, at] = jnp.where(near_first, 0.0, colors[c]) + jnp.where(
+                own_first, 0.0, after * own_color
+            )
+        out_ref[w, 3, at] = ahead * jnp.where(near_first, through, 1.0)
+        back[w, 3, at] = after * jnp.where(own_first, 1.0, own_through)
+
+    def far_layer(w, top):
+        at = pl.ds(top, tile)
+        colors, through = march(
+            w, top, 1 - z, far, 2, m_ref, 1 + far, [out_ref[w, c, at] for c in range(3)],
             out_ref[w, 3, at],
         )
         for c in range(3):
@@ -640,10 +661,11 @@
     views(own_layer)
     sided(lambda mine: ending(mine, 1))
     each(bz + 1 - 3 * z, bz + 2 - 3 * z)
+    views(near_layer)
     sided(lambda mine: ending(mine, 2))
     for k in range(2):
         slopes((1 - z) * (depth - 2) + k, 0)
-    views(other_layer)
+    views(far_layer)
     sided(lambda mine: steps[mine][3]())
 
 
@@ -675,6 +697,7 @@
             pltpu.VMEM((bz, rows, LANES), f32),
             pltpu.VMEM((depth + 2, tall, LANES), f32),
             pltpu.VMEM((bz, tall, LANES), f32),
+            pltpu.VMEM((bz - 2, tall, LANES), f32),
             pltpu.VMEM((2, got, LANES), f32),
             pltpu.VMEM((2, 2, SUB, LANES), f32),
             pltpu.VMEM((sent, LANES), f32),

time: 12.4 us -> 12.2 us (0.984)
  Pallas kernels: 11.5 us -> 11.2 us
    pallas_call x1, Pallas kernels: 11.5 us -> 11.2 us  [two_bricks(): pl.pallas_call(functools.partial(render, dims), out_shape=jax.ShapeDtypeS...]
where the time goes in v9:
time: 12.2 us; the launch traced here: 12.1 us
  Pallas kernels  11.2 us (92%)
  local copies, waits for them, and re-layouts  0.8 us (7%)
    pallas_call x1, Pallas kernels, two_bricks(): pl.pallas_call(functools.partial(render, dims), out_shape=jax.ShapeDtypeS...  11.2 us
    unnamed x1, local copies, waits for them, and re-layouts  0.8 us

profile of v9, /device:TPU:9, one launch (start us, length us, event | category | flops | bytes accessed | tf_op | source)
XLA Modules:
  0.0 12.1 jit_solution(12331147087369799398)
XLA Ops:
  0.0 11.2 %render.1 = f32[4,4,64,128]{3,2,1,0:T(8,128)S(1)} custom-call(f32[4,3]{1,0:T(4,128)} %light_in.1, f32[2,3]{1,0:T(2,128)} %bitcast.10, f32[4]{0:T(128)} %rate_in.1, s32[4,2,8]{2,1,0:T(2,128)} %bitcast.8, s32[2,2,4]{2,1,0:T(2,128)} %bitcast.9, s32[2,4]{1,0:T(2,128)} %bitcast.11, f32[4,128,128]{2,1,0:T(8,128)} %p_ref.1), custom_call_target="tpu_custom_call" | custom-call | tf_op jit(solution)/shard_map/render/pallas_call | solution.py:690
  11.3 0.8 %copy.10 = f32[4,4,1,64,128]{4,3,2,1,0:T(8,128)} copy(f32[4,4,1,64,128]{4,3,2,1,0:T(8,128)S(1)} %bitcast.7) | data formatting | bytes 1048576

commit v10 on v9

--- a/solution.py
+++ b/solution.py
@@ -616,7 +616,9 @@
 
     def own_layer(w, top):
         at = pl.ds(top, tile)
-        colors, through = march(w, top, z, z * bz, bz, own_ref, 0, [zero] * 3, zero + 1.0)
+        colors, through = march(
+            w, top, z, z * (bz + 1), bz - 1, own_ref, z, [zero] * 3, zero + 1.0
+        )
         for c in range(3):
             back[w, c, at] = colors[c]
         back[w, 3, at] = through
@@ -627,11 +629,17 @@
             w, top, 1 - z, near, early, near_ref, 0, [zero] * 3, zero + 1.0
         )
         own_first, near_first = order[0, w] == z, z == 0
-        own_through = back[w, 3, at]
+        edge_colors, edge_through = march(
+            w, top, z, bz - 1 + z, 1, own_ref, (1 - z) * (bz - 1), [zero] * 3, zero + 1.0
+        )
+        inner_through = back[w, 3, at]
+        own_through = inner_through * edge_through
+        of_inner = jnp.where(near_first, 1.0, edge_through)
+        of_edge = jnp.where(near_first, inner_through, 1.0)
         ahead = jnp.where(own_first, own_through, 1.0)
         after = jnp.where(near_first, 1.0, through)
         for c in range(3):
-            own_color = back[w, c, at]
+            own_color = of_inner * back[w, c, at] + of_edge * edge_colors[c]
             out_ref[w, c, at] = jnp.where(own_first, own_color, 0.0) + jnp.where(
                 near_first, ahead * colors[c], 0.0
             )
@@ -655,10 +663,10 @@
         lax.fori_loop(start, stop, slopes, 0)
 
     each(z * (bz + 1), z * (bz + 1) + bz - 1)
+    views(own_layer)
     sided(middle)
     for k in range(2):
         slopes(bz - 1 + k, 0)
-    views(own_layer)
     sided(lambda mine: ending(mine, 1))
     each(bz + 1 - 3 * z, bz + 2 - 3 * z)
     views(near_layer)

time: 12.2 us -> 12.4 us (1.016)
  Pallas kernels: 11.2 us -> 11.4 us
    pallas_call x1, Pallas kernels: 11.2 us -> 11.4 us  [two_bricks(): pl.pallas_call(functools.partial(render, dims), out_shape=jax.ShapeDtypeS...]
where the time goes in v10:
time: 12.4 us; the launch traced here: 12.2 us
  Pallas kernels  11.4 us (92%)
  local copies, waits for them, and re-layouts  0.8 us (6%)
    pallas_call x1, Pallas kernels, two_bricks(): pl.pallas_call(functools.partial(render, dims), out_shape=jax.ShapeDtypeS...  11.4 us
    unnamed x1, local copies, waits for them, and re-layouts  0.8 us

profile of v10, /device:TPU:9, one launch (start us, length us, event | category | flops | bytes accessed | tf_op | source)
XLA Modules:
  0.0 12.2 jit_solution(9858300230922021878)
XLA Ops:
  0.0 11.4 %render.1 = f32[4,4,64,128]{3,2,1,0:T(8,128)S(1)} custom-call(f32[4,3]{1,0:T(4,128)} %light_in.1, f32[2,3]{1,0:T(2,128)} %bitcast.10, f32[4]{0:T(128)} %rate_in.1, s32[4,2,8]{2,1,0:T(2,128)} %bitcast.8, s32[2,2,4]{2,1,0:T(2,128)} %bitcast.9, s32[2,4]{1,0:T(2,128)} %bitcast.11, f32[4,128,128]{2,1,0:T(8,128)} %p_ref.1), custom_call_target="tpu_custom_call" | custom-call | tf_op jit(solution)/shard_map/render/pallas_call | solution.py:698
  11.4 0.8 %copy.10 = f32[4,4,1,64,128]{4,3,2,1,0:T(8,128)} copy(f32[4,4,1,64,128]{4,3,2,1,0:T(8,128)S(1)} %bitcast.7) | data formatting | bytes 1048576

commit v11 on v10

--- a/solution.py
+++ b/solution.py
@@ -264,6 +264,7 @@
     mains, own_halo, halos = (
         (routes[2], routes[1], routes[3]) if mine == 0 else (routes[0], routes[3], routes[1])
     )
+    first, second = (halos, mains) if mine == 0 else (mains, halos)
     next_ones = [1 + there.astype(jnp.int32) for there in (has_down, has_up)]
 
     def send_first():
@@ -286,10 +287,10 @@
         if mine == 1:
             heard(BELOW, has_down, 1)
             start(rows_out(halos))
-        start(rows_out(halos, 1) + rows_out(mains, 1))
+        start(rows_out(first, 1) + rows_out(second, 1))
         heard(ACROSS, has_right, next_ones[1 - mine])
         start(cols_sent(False))
-        start(rows_out(halos, 2) + rows_out(mains, 2))
+        start(rows_out(first, 2) + rows_out(second, 2))
 
     def receive(brick, parts, sides):
         pairs = []

time: 12.4 us -> 12.1 us (0.976)
  the two profiles are of different devices: /device:TPU:9 before, /device:TPU:12 now
where the time goes in v11:
time: 12.1 us; the launch traced here: 11.9 us
  Pallas kernels  11.1 us (92%)
  local copies, waits for them, and re-layouts  0.8 us (7%)
    pallas_call x1, Pallas kernels, two_bricks(): pl.pallas_call(functools.partial(render, dims), out_shape=jax.ShapeDtypeS...  11.1 us
    unnamed x1, local copies, waits for them, and re-layouts  0.8 us

profile of v11, /device:TPU:12, one launch (start us, length us, event | category | flops | bytes accessed | tf_op | source)
XLA Modules:
  0.0 11.9 jit_solution(3504618484781103837)
XLA Ops:
  0.0 11.1 %render.1 = f32[4,4,64,128]{3,2,1,0:T(8,128)S(1)} custom-call(f32[4,3]{1,0:T(4,128)} %light_in.1, f32[2,3]{1,0:T(2,128)} %bitcast.10, f32[4]{0:T(128)} %rate_in.1, s32[4,2,8]{2,1,0:T(2,128)} %bitcast.8, s32[2,2,4]{2,1,0:T(2,128)} %bitcast.9, s32[2,4]{1,0:T(2,128)} %bitcast.11, f32[4,128,128]{2,1,0:T(8,128)} %p_ref.1), custom_call_target="tpu_custom_call" | custom-call | tf_op jit(solution)/shard_map/render/pallas_call | solution.py:699
  11.1 0.8 %copy.10 = f32[4,4,1,64,128]{4,3,2,1,0:T(8,128)} copy(f32[4,4,1,64,128]{4,3,2,1,0:T(8,128)S(1)} %bitcast.7) | data formatting | bytes 1048576

commit v12 on v11

--- a/solution.py
+++ b/solution.py
@@ -669,7 +669,7 @@
     for k in range(2):
         slopes(bz - 1 + k, 0)
     sided(lambda mine: ending(mine, 1))
-    each(bz + 1 - 3 * z, bz + 2 - 3 * z)
+    slopes(bz + 1 - 3 * z, 0)
     views(near_layer)
     sided(lambda mine: ending(mine, 2))
     for k in range(2):

time: 12.1 us -> 12.1 us (level)
  no operation moved by 1% of the time
where the time goes in v12:
time: 12.1 us; the launch traced here: 11.9 us
  Pallas kernels  11.1 us (92%)
  local copies, waits for them, and re-layouts  0.8 us (7%)
    pallas_call x1, Pallas kernels, two_bricks(): pl.pallas_call(functools.partial(render, dims), out_shape=jax.ShapeDtypeS...  11.1 us
    unnamed x1, local copies, waits for them, and re-layouts  0.8 us

profile of v12, /device:TPU:12, one launch (start us, length us, event | category | flops | bytes accessed | tf_op | source)
XLA Modules:
  0.0 11.9 jit_solution(13140598917874991183)
XLA Ops:
  0.0 11.1 %render.1 = f32[4,4,64,128]{3,2,1,0:T(8,128)S(1)} custom-call(f32[4,3]{1,0:T(4,128)} %light_in.1, f32[2,3]{1,0:T(2,128)} %bitcast.10, f32[4]{0:T(128)} %rate_in.1, s32[4,2,8]{2,1,0:T(2,128)} %bitcast.8, s32[2,2,4]{2,1,0:T(2,128)} %bitcast.9, s32[2,4]{1,0:T(2,128)} %bitcast.11, f32[4,128,128]{2,1,0:T(8,128)} %p_ref.1), custom_call_target="tpu_custom_call" | custom-call | tf_op jit(solution)/shard_map/render/pallas_call | solution.py:699
  11.1 0.8 %copy.10 = f32[4,4,1,64,128]{4,3,2,1,0:T(8,128)} copy(f32[4,4,1,64,128]{4,3,2,1,0:T(8,128)S(1)} %bitcast.7) | data formatting | bytes 1048576

commit v13 on v12

--- a/solution.py
+++ b/solution.py
@@ -290,7 +290,7 @@
         start(rows_out(first, 1) + rows_out(second, 1))
         heard(ACROSS, has_right, next_ones[1 - mine])
         start(cols_sent(False))
-        start(rows_out(first, 2) + rows_out(second, 2))
+        start(rows_out(halos, 2) + rows_out(mains, 2))
 
     def receive(brick, parts, sides):
         pairs = []

time: 12.1 us -> 12.2 us (level)
  the two profiles are of different devices: /device:TPU:12 before, /device:TPU:9 now
where the time goes in v13:
time: 12.2 us; the launch traced here: 12 us
  Pallas kernels  11.2 us (92%)
  local copies, waits for them, and re-layouts  0.8 us (7%)
    pallas_call x1, Pallas kernels, two_bricks(): pl.pallas_call(functools.partial(render, dims), out_shape=jax.ShapeDtypeS...  11.2 us
    unnamed x1, local copies, waits for them, and re-layouts  0.8 us

profile of v13, /device:TPU:9, one launch (start us, length us, event | category | flops | bytes accessed | tf_op | source)
XLA Modules:
  0.0 12.0 jit_solution(8294680551903568755)
XLA Ops:
  0.0 11.2 %render.1 = f32[4,4,64,128]{3,2,1,0:T(8,128)S(1)} custom-call(f32[4,3]{1,0:T(4,128)} %light_in.1, f32[2,3]{1,0:T(2,128)} %bitcast.10, f32[4]{0:T(128)} %rate_in.1, s32[4,2,8]{2,1,0:T(2,128)} %bitcast.8, s32[2,2,4]{2,1,0:T(2,128)} %bitcast.9, s32[2,4]{1,0:T(2,128)} %bitcast.11, f32[4,128,128]{2,1,0:T(8,128)} %p_ref.1), custom_call_target="tpu_custom_call" | custom-call | tf_op jit(solution)/shard_map/render/pallas_call | solution.py:699
  11.2 0.8 %copy.10 = f32[4,4,1,64,128]{4,3,2,1,0:T(8,128)} copy(f32[4,4,1,64,128]{4,3,2,1,0:T(8,128)S(1)} %bitcast.7) | data formatting | bytes 1048576
